TPU v7x, 32 devices: a whole 2x2x4 slice. The times are simulated.
32 devices in a mesh: replica: 2 (over y), tensor: 16 (over z, x, core).
Axes of the slice: x: 2, y: 2, z: 4, core: 2. Of those that a mesh axis runs over, the one named last changes fastest.
Arguments:
- tokens: bfloat16 [256, 2560], P('replica', 'tensor'), may hold values from -6 to 6
- next_tokens: bfloat16 [128, 2560], P('replica', 'tensor'), may hold values from -6 to 6
- cotangent: bfloat16 [256, 2560], P('replica', 'tensor'), may hold values from -0.5 to 0.5
- gate_weight: bfloat16 [2560, 14336], P(None, 'tensor'), may hold values from -0.125 to 0.125
- up_weight: bfloat16 [2560, 14336], P(None, 'tensor'), may hold values from -0.125 to 0.125
- down_weight: bfloat16 [14336, 2560], P('tensor'), may hold values from -0.046875 to 0.046875
- momentum: bfloat16 [2, 14336, 2560], P('replica', 'tensor'), may hold values from -6 to 6
- indices: int32 [2, 224, 40, 32], P(None, 'tensor'), may hold values from 0 to 4095, as said below
Outputs:
- output: bfloat16 [128, 2560], P(('replica', 'tensor'))
- new_momentum: bfloat16 [2, 14336, 2560], P('replica', 'tensor')
Inputs may be any that keep to these rules, and one draw needn't show every extreme that they name: Within one replica and tile the 32 indices are distinct; the n-th lies in the range from n * 64 * 2 to (n + 1) * 64 * 2 - 1.
All inputs are finite; a program needn't handle non-finite values.
Results may differ from a plain program's by a relative error of at most 0.017.
Values may be sent and summed in bfloat16 or wider, within the bound.
A program may use at most 128 MiB of HBM per device.

v0:
```python
import jax
import jax.numpy as jnp
from jax import lax
from jax.sharding import PartitionSpec as P

TILE = 64


BETA_DECAY = 0.9
STEP_RATE = 0.1


def cosine_table():
    freq = jnp.arange(TILE, dtype=jnp.float32)[:, None]
    place = jnp.arange(TILE, dtype=jnp.float32)[None, :]
    table = jnp.cos(jnp.pi * (2.0 * place + 1.0) * freq / (2.0 * TILE))
    factor = jnp.where(freq == 0.0, jnp.sqrt(1.0 / TILE), jnp.sqrt(2.0 / TILE))
    return table * factor


def forward_tiles(field, table):
    height, breadth = field.shape
    blocks = field.reshape(height // TILE, TILE, breadth // TILE, TILE)
    spectrum = jnp.einsum("ak,xkyl,bl->xyab", table, blocks, table, precision=lax.Precision.HIGHEST)
    return spectrum.reshape(height // TILE, breadth // TILE, TILE * TILE)


def inverse_tiles(spectrum, table):
    tile_rows, tile_cols, _ = spectrum.shape
    blocks = spectrum.reshape(tile_rows, tile_cols, TILE, TILE)
    field = jnp.einsum("ak,xyab,bl->xkyl", table, blocks, table, precision=lax.Precision.HIGHEST)
    return field.reshape(tile_rows * TILE, tile_cols * TILE)


def one_hot_slots(where):
    keep_count = where.shape[-1]
    stride = TILE * TILE // keep_count
    offset = where - jnp.arange(keep_count, dtype=jnp.int32) * stride
    slots = jnp.arange(stride, dtype=jnp.int32)
    return (offset[..., None] == slots).astype(jnp.float32)


def pick_values(spectrum, where):
    tile_rows, tile_cols, keep_count = where.shape
    grid = spectrum.reshape(tile_rows, tile_cols, keep_count, TILE * TILE // keep_count)
    return jnp.sum(grid * one_hot_slots(where), axis=3)


def place_values(values, where):
    tile_rows, tile_cols, _ = where.shape
    placed = values[..., None] * one_hot_slots(where)
    return placed.reshape(tile_rows, tile_cols, TILE * TILE)


def place_listed(listed, where):
    replicas = where.shape[0]
    tile_rows, tile_cols = (where.shape[1], where.shape[2])

    def add_replica(step, dense):
        values = lax.dynamic_index_in_dim(listed, step, 0, keepdims=False).astype(jnp.float32)
        spots = lax.dynamic_index_in_dim(where, step, 0, keepdims=False)
        return dense + place_values(values, spots)

    dense = jnp.zeros((tile_rows, tile_cols, TILE * TILE), jnp.float32)
    return lax.fori_loop(0, replicas, add_replica, dense)


def swiglu(inputs, gate_weight, up_weight):
    gate = jnp.dot(inputs, gate_weight, preferred_element_type=jnp.float32)
    upper = jnp.dot(inputs, up_weight, preferred_element_type=jnp.float32)
    return (jax.nn.silu(gate) * upper).astype(jnp.bfloat16)


def on_device(
    tokens, next_tokens, cotangent, gate_weight, up_weight, down_weight, momentum, indices
):
    table = cosine_table()
    whole, whole_next, whole_grads = (
        lax.all_gather(tokens, "tensor", axis=1, tiled=True),
        lax.all_gather(next_tokens, "tensor", axis=1, tiled=True),
        lax.all_gather(cotangent, "tensor", axis=1, tiled=True),
    )
    hidden = swiglu(whole, gate_weight, up_weight)
    grad = lax.dot_general(
        hidden, whole_grads, (((0,), (0,)), ((), ())), preferred_element_type=jnp.float32
    )
    moment = BETA_DECAY * momentum[0].astype(jnp.float32) + grad
    spectrum = forward_tiles(moment, table)
    replica = lax.axis_index("replica")
    replicas = lax.axis_size("replica")
    own_where = lax.dynamic_index_in_dim(indices, replica, 0, keepdims=False)
    sent = pick_values(spectrum, own_where).astype(jnp.bfloat16)
    own = place_values(sent.astype(jnp.float32), own_where)
    kept = (moment - inverse_tiles(own, table)).astype(jnp.bfloat16)
    next_hidden = swiglu(whole_next, gate_weight, up_weight)
    share = spectrum.shape[1] // replicas
    first = replica * share
    listed = lax.all_gather(sent[None], "replica", axis=0, tiled=True)
    total = place_listed(
        lax.dynamic_slice_in_dim(listed, first, share, 2),
        lax.dynamic_slice_in_dim(indices, first, share, 2),
    )
    update = inverse_tiles(total, table) / replicas
    down_share = lax.dynamic_slice_in_dim(down_weight, first * TILE, share * TILE, 1)
    new_share = (down_share.astype(jnp.float32) - STEP_RATE * update).astype(jnp.bfloat16)
    new_down = lax.all_gather(new_share, "replica", axis=1, tiled=True)
    output = lax.psum_scatter(
        jnp.dot(next_hidden, new_down, preferred_element_type=jnp.float32).astype(jnp.bfloat16),
        "tensor",
        scatter_dimension=0,
        tiled=True,
    )
    return (output, kept[None])


def solution(mesh):
    return jax.shard_map(
        on_device,
        mesh=mesh,
        in_specs=(
            P("replica", "tensor"),
            P("replica", "tensor"),
            P("replica", "tensor"),
            P(None, "tensor"),
            P(None, "tensor"),
            P("tensor", None),
            P("replica", "tensor", None),
            P(None, "tensor", None, None),
        ),
        out_specs=(P(("replica", "tensor"), None), P("replica", "tensor", None)),
        check_vma=False,
    )
```

profile of v0, /device:TPU:0, one launch (start us, length us, event | category | flops | bytes accessed | tf_op | source)
XLA Modules:
  0.0 497.5 jit_solution(8891392778174290097)
XLA Ops:
  7.3 25.3 %all_gather.16 = bf16[128,2560]{0,1:T(8,128)(2,1)S(1)} all-gather(bf16[128,160]{0,1:T(8,128)(2,1)} %param.10), channel_id=1, replica_groups=mesh['replica'=2,'tensor'=16] {'tensor'}, dimensions={1}, use_global_device_ids=true | all-gather | bytes 696320 | tf_op jit(solution)/shard_map/all_gather | solution.py:79
  32.6 19.5 %all_gather.17 = bf16[128,2560]{0,1:T(8,128)(2,1)S(1)} all-gather(bf16[128,160]{0,1:T(8,128)(2,1)} %param.12), channel_id=1, replica_groups=mesh['replica'=2,'tensor'=16] {'tensor'}, dimensions={1}, use_global_device_ids=true | all-gather | bytes 696320 | tf_op jit(solution)/shard_map/all_gather | solution.py:81
  52.1 3.2 fusion.59
  55.2 8.5 %bitcast_add_fusion = f32[896,2560]{1,0:T(8,128)} fusion(bf16[1,896,2560]{2,1,0:T(8,128)(2,1)} %param.16, bf16[128,2560]{0,1:T(8,128)(2,1)S(1)} %all_gather.17, bf16[128,2560]{0,1:T(8,128)(2,1)S(1)} %all_gather.16, bf16[2560,896]{1,0:T(8,128)(2,1)} %param.14, f32[128,896]{1,0:T(8,128)S(1)} %fusion.59), kind=kOutput, calls=%fused_computation.13 | convolution fusion | flops 1181974528 | bytes 20119552 | tf_op jit(solution)/shard_map/dot_general | solution.py:84
  63.7 14.0 %reshape.98 = f32[14,64,40,64]{3,2,1,0:T(8,128)} reshape(f32[896,2560]{1,0:T(8,128)} %bitcast_add_fusion) | data formatting | bytes 18350080 | tf_op jit(solution)/shard_map/reshape | solution.py:23
  78.0 0.2 copy.36
  78.3 35.8 %fusion.2 = f32[14,40,64,64]{3,2,1,0:T(8,128)} fusion(f32[14,64,40,64]{3,2,1,0:T(8,128)} %reshape.98, f32[64]{0:T(128)S(1)} %get-tuple-element.113, f32[64]{0:T(128)S(1)} %get-tuple-element.114), kind=kOutput, calls=%fused_computation.9 | convolution fusion | flops 1761619968 | bytes 18350592 | tf_op jit(solution)/shard_map/ak,xkyl,bl->xyab/dot_general | solution.py:24
  114.1 24.3 %fusion = f32[14,40,64]{2,1,0:T(8,128)S(1)} fusion(s32[64,64]{0,1:T(8,128)S(1)} %copy.37, s32[14,40,64]{2,1,0:T(8,128)S(1)} %copy.36, f32[14,40,64,64]{3,2,1,0:T(8,128)} %fusion.2, f32[64]{0:T(128)S(1)} %get-tuple-element.113, f32[64]{0:T(128)S(1)} %get-tuple-element.114), kind=kOutput, calls=%fused_computation.7 | convolution fusion | flops 1768465408 | bytes 9478656 | tf_op jit(solution)/shard_map/ak,xkyl,bl->xyab/dot_general | solution.py:24
  138.4 0.2 copy.39
  138.6 0.6 reduce_sum.18
  139.2 6.1 %all-gather = bf16[28,40,32]{1,2,0:T(8,128)(2,1)S(1)} all-gather(bf16[14,40,32]{1,2,0:T(8,128)(2,1)S(1)} %reduce_sum.18), channel_id=2, replica_groups=mesh['replica'=2,'tensor'=16] {'replica'}, dimensions={0}, use_global_device_ids=true | all-gather | bytes 107520 | tf_op jit(solution)/shard_map/all_gather | solution.py:98
  145.3 0.2 constant_dynamic-slice_fusion.1
  145.6 0.3 copy.40
  145.9 0.3 copy.53
  146.2 54.2 %while.14 = (s32[]{:T(128)}, f32[14,20,4096]{2,0,1:T(8,128)}, s32[2,14,20,32]{3,1,2,0:T(8,128)S(1)}, bf16[2,14,20,32]{3,1,2,0:T(8,128)(2,1)S(1)}, s32[]{:T(128)}, /*index=5*/s32[]{:T(128)}) while((s32[]{:T(128)}, f32[14,20,4096]{2,0,1:T(8,128)}, s32[2,14,20,32]{3,1,2,0:T(8,128)S(1)}, bf16[2,14,20,32]{3,1,2,0:T(8,128)(2,1)S(1)}, ...), condition=%wide.region_3.4_spmd.clone, body=%wide.region_2.3_spmd.clone.sunk | while | flops 4605475 | bytes 46105428 | solution.py:65
  146.7 4.3 eq.144
  151.0 5.3 %eq.145 = s32[14,20,4096]{2,0,1:T(8,128)} reshape(s32[14,20,32,128]{3,2,0,1:T(8,128)} %eq.144) | data formatting | bytes 9175040 | tf_op jit(solution)/shard_map/while/body/eval_jaxpr/eq | solution.py:40
  156.3 2.8 mul.389
  159.1 5.3 %mul.390 = f32[14,20,4096]{2,0,1:T(8,128)} reshape(f32[14,20,32,128]{3,2,0,1:T(8,128)} %mul.389) | data formatting | bytes 9175040 | tf_op jit(solution)/shard_map/while/body/eval_jaxpr/mul | solution.py:51
  164.4 8.4 %select_add_fusion.2 = f32[14,20,4096]{2,0,1:T(8,128)} fusion(f32[14,20,4096]{2,0,1:T(8,128)} %get-tuple-element.147, f32[14,20,4096]{2,0,1:T(8,128)} %mul.390, s32[14,20,4096]{2,0,1:T(8,128)} %eq.145, s32[4096]{0:T(1024)S(1)} %iota_bitcast_fusion.2, pred[]{:T(512)S(6)} %compare.3), kind=kLoop, calls=%fused_computation.clone.1 | loop fusion | flops 4587520 | bytes 18366464 | tf_op jit(solution)/shard_map/while/body/eval_jaxpr/add | solution.py:62
  172.8 4.3 eq.144
  177.1 5.3 %eq.145 = s32[14,20,4096]{2,0,1:T(8,128)} reshape(s32[14,20,32,128]{3,2,0,1:T(8,128)} %eq.144) | data formatting | bytes 9175040 | tf_op jit(solution)/shard_map/while/body/eval_jaxpr/eq | solution.py:40
  182.5 2.8 mul.389
  185.3 5.3 %mul.390 = f32[14,20,4096]{2,0,1:T(8,128)} reshape(f32[14,20,32,128]{3,2,0,1:T(8,128)} %mul.389) | data formatting | bytes 9175040 | tf_op jit(solution)/shard_map/while/body/eval_jaxpr/mul | solution.py:51
  190.6 9.9 %select_add_fusion.2 = f32[14,20,4096]{2,0,1:T(8,128)} fusion(f32[14,20,4096]{2,0,1:T(8,128)} %get-tuple-element.147, f32[14,20,4096]{2,0,1:T(8,128)} %mul.390, s32[14,20,4096]{2,0,1:T(8,128)} %eq.145, s32[4096]{0:T(1024)S(1)} %iota_bitcast_fusion.2, pred[]{:T(512)S(6)} %compare.3), kind=kLoop, calls=%fused_computation.clone.1 | loop fusion | flops 4587520 | bytes 18366464 | tf_op jit(solution)/shard_map/while/body/eval_jaxpr/add | solution.py:62
  200.4 9.1 %reshape.99 = f32[14,20,64,64]{3,2,0,1:T(8,128)} reshape(f32[14,20,4096]{2,0,1:T(8,128)} %get-tuple-element.81) | data formatting | bytes 9175040 | tf_op jit(solution)/shard_map/reshape | solution.py:30
  209.5 11.8 %fusion.4 = f32[14,20,64,64]{2,3,1,0:T(8,128)S(1)} fusion(f32[14,20,64,64]{3,2,0,1:T(8,128)} %reshape.99, f32[64]{0:T(128)S(1)} %get-tuple-element.113, f32[64]{0:T(128)S(1)} %get-tuple-element.114), kind=kOutput, calls=%fused_computation.11 | convolution fusion | flops 880816128 | bytes 9175552 | tf_op jit(solution)/shard_map/ak,xyab,bl->xkyl/dot_general | solution.py:31
  221.3 10.0 %multiply_bitcast_fusion = f32[14,64,20,64]{3,1,2,0:T(8,128)} fusion(f32[14,20,64,64]{2,3,1,0:T(8,128)S(1)} %fusion.4, f32[64]{0:T(128)S(1)} %get-tuple-element.113, f32[64]{0:T(128)S(1)} %get-tuple-element.114), kind=kOutput, calls=%fused_computation.16 | convolution fusion | flops 881963008 | bytes 9175552 | tf_op jit(solution)/shard_map/ak,xyab,bl->xkyl/dot_general | solution.py:31
  231.3 11.4 %copy.43 = f32[14,64,20,64]{1,0,3,2:T(8,128)} copy(f32[14,64,20,64]{3,1,2,0:T(8,128)} %multiply_bitcast_fusion) | data formatting | bytes 9175040 | tf_op jit(solution)/shard_map/mul | solution.py:105
  242.7 9.5 %mul.231 = f32[896,1280]{0,1:T(8,128)} reshape(f32[14,64,20,64]{1,0,3,2:T(8,128)} %copy.43) | data formatting | bytes 9175040 | tf_op jit(solution)/shard_map/mul | solution.py:105
  252.3 3.2 constant_dynamic-slice_fusion.2
  255.4 3.2 copy.52
  258.6 4.1 subtract_convert_fusion.1
  262.8 20.4 %all-gather.1 = bf16[16,160,64]{1,2,0:T(8,128)(2,1)S(1)} all-gather(bf16[1,160,64]{1,2,0:T(8,128)(2,1)S(1)} %bitcast.81), channel_id=1, replica_groups=mesh['replica'=2,'tensor'=16] {'tensor'}, dimensions={0}, use_global_device_ids=true | all-gather | bytes 348160 | tf_op jit(solution)/shard_map/all_gather | solution.py:80
  283.2 0.3 copy.33
  283.5 0.7 reshape.104
  284.2 0.2 mul.232
  284.4 0.2 copy.44
  284.6 53.7 %fusion.1 = f32[14,40,64,64]{2,3,1,0:T(8,128)S(1)} fusion(f32[14,40,64]{2,1,0:T(8,128)S(1)} %copy.44, s32[64,64]{0,1:T(8,128)S(1)} %copy.37, s32[14,40,64]{2,1,0:T(8,128)S(1)} %copy.36, f32[64]{0:T(128)S(1)} %get-tuple-element.113, f32[64]{0:T(128)S(1)} %get-tuple-element.114), kind=kOutput, calls=%fused_computation.8 | convolution fusion | flops 1766207488 | bytes 9478656 | tf_op jit(solution)/shard_map/ak,xyab,bl->xkyl/dot_general | solution.py:31
  338.2 17.6 %convolution_bitcast_fusion = f32[14,64,40,64]{3,1,2,0:T(8,128)} fusion(f32[14,40,64,64]{2,3,1,0:T(8,128)S(1)} %fusion.1, f32[64]{0:T(128)S(1)} %get-tuple-element.113, f32[64]{0:T(128)S(1)} %get-tuple-element.114), kind=kOutput, calls=%fused_computation.20 | convolution fusion | flops 1761619968 | bytes 18350592 | tf_op jit(solution)/shard_map/ak,xyab,bl->xkyl/dot_general | solution.py:31
  355.8 20.5 %copy.46 = f32[14,64,40,64]{3,2,1,0:T(8,128)} copy(f32[14,64,40,64]{3,1,2,0:T(8,128)} %convolution_bitcast_fusion) | data formatting | bytes 18350080 | tf_op jit(solution)/shard_map/ak,xyab,bl->xkyl/transpose | solution.py:31
  376.4 15.7 %reshape.100 = f32[896,2560]{1,0:T(8,128)} reshape(f32[14,64,40,64]{3,2,1,0:T(8,128)} %copy.46) | data formatting | bytes 18350080 | tf_op jit(solution)/shard_map/reshape | solution.py:32
  392.0 3.2 fusion.58
  395.2 6.7 %convolution_convert_fusion = bf16[64,2560]{1,0:T(8,128)(2,1)} fusion(bf16[896,2560]{0,1:T(8,128)(2,1)} %all-gather.4.cloned.1.call-done, bf16[2560,64]{0,1:T(8,128)(2,1)S(1)} %reshape.104, bf16[2560,896]{1,0:T(8,128)(2,1)} %param.14, f32[64,896]{1,0:T(8,128)S(1)} %fusion.58), kind=kOutput, calls=%fused_computation.23 | convolution fusion | flops 587710464 | bytes 10059776 | tf_op jit(solution)/shard_map/dot_general | solution.py:108
  401.9 9.9 %fusion.10 = bf16[1,896,2560]{2,1,0:T(8,128)(2,1)} fusion(f32[896,2560]{1,0:T(8,128)} %bitcast_add_fusion, f32[896,2560]{1,0:T(8,128)} %reshape.100), kind=kLoop, calls=%fused_computation.21 | loop fusion | flops 4587520 | bytes 22937600 | tf_op jit(solution)/shard_map/broadcast_in_dim | solution.py:113
  411.9 0.6 dynamic-slice
  413.1 75.7 %all-reduce.3.cloned.1.call-done = bf16[64,2560]{1,0:T(8,128)(2,1)} async-done(((bf16[64,2560]{1,0:T(8,128)(2,1)}), bf16[64,2560]{1,0:T(8,128)(2,1)}) %all-reduce.3.cloned.1.call-update) | async-done | bytes 327696
  488.8 1.4 constant_dynamic-slice_fusion.3
  (28 shorter events, 0.7 us)
Async XLA Ops:
  7.2 388.1 %all-gather.4.cloned.1.call-start = ((), (), s32[]{:S(2)}) async-start(), calls=%async_computation | async-start | bytes 6881280 | tf_op jit(solution)/shard_map/all_gather | solution.py:106
  63.7 14.0 %copy-start = (s32[2,14,40,32]{2,3,1,0:T(8,128)S(1)}, s32[2,14,40,32]{2,3,1,0:T(8,128)}, u32[]{:S(2)}) copy-start(s32[2,14,40,32]{2,3,1,0:T(8,128)} %param.17) | copy-start | bytes 430084
  258.6 4.2 copy-start.1
  262.7 226.1 %all-reduce.3.cloned.1.call-start = ((), (), s32[]{:S(2)}) async-start(), calls=%async_computation.1 | async-start | bytes 655360
  401.9 10.0 %copy-start.2 = (u32[32]{0:T(128)S(1)}, u32[32]{0:T(128)}, u32[]{:S(2)}) copy-start(u32[32]{0:T(128)} %constant.99) | copy-start | bytes 388
Sparse Core Ops, SparseCore 0:
  262.9 59.6 all-gather.3
  402.1 86.7 all-reduce.2
where the time goes:
time: 508 us; the launch traced here: 497 us
  matrix products  175 us (34%)
  local copies, waits for them, and re-layouts  127 us (25%)
  waiting for transfers between devices  75.7 us (15%)
  blocking collectives  71.2 us (14%)
  other arithmetic  33.1 us (7%)
  between operations  15.3 us (3%)
    dot_general x4, matrix products, inverse_tiles(): jnp.einsum('ak,xyab,bl->xkyl', table, blocks, table, precision=lax.Precis...  93 us
    unnamed x3, waiting for transfers between devices  75.7 us
    dot_general x2, matrix products, forward_tiles(): jnp.einsum('ak,xkyl,bl->xyab', table, blocks, table, precision=lax.Precis...  60.1 us
    all_gather x1, blocking collectives, on_device(): lax.all_gather(tokens, 'tensor', axis=1, tiled=True)  25.3 us
    mul x2, local copies, waits for them, and re-layouts, on_device(): STEP_RATE * update  21 us
    transpose x1, local copies, waits for them, and re-layouts, inverse_tiles(): jnp.einsum('ak,xyab,bl->xkyl', table, blocks, table, precision=lax.Precis...  20.5 us
    all_gather x1, blocking collectives, on_device(): lax.all_gather(next_tokens, 'tensor', axis=1, tiled=True)  20.4 us
    eq x10, local copies, waits for them, and re-layouts, one_hot_slots(): return (offset[..., None] == slots).astype(jnp.float32)  19.7 us
  transfers between devices with their start and end apart: 2, of which 1 were waited for; matrix products, arithmetic and copies ran while one was open for 25% of the time, Pallas kernels for 0%

commit v1 on v0

v1 whole, which is shorter than its diff:
```python
import functools

import jax
import jax.numpy as jnp
import numpy as np
from jax import lax
from jax.experimental import pallas as pl
from jax.experimental.pallas import tpu as pltpu
from jax.sharding import PartitionSpec as P

TILE = 64
BETA_DECAY = 0.9
STEP_RATE = 0.1
MESH = pl.DeviceIdType.MESH
VMEM = pl.BlockSpec(memory_space=pltpu.VMEM)


def cosine_table():
    freq = np.arange(TILE)[:, None]
    place = np.arange(TILE)[None, :]
    table = np.cos(np.pi * (2.0 * place + 1.0) * freq / (2.0 * TILE))
    return table * np.where(freq == 0, np.sqrt(1.0 / TILE), np.sqrt(2.0 / TILE))


def split_bf16(table):
    high = jnp.asarray(table, jnp.float32).astype(jnp.bfloat16)
    rest = jnp.asarray(table, jnp.float32) - high.astype(jnp.float32)
    return high, rest.astype(jnp.bfloat16)


def tables(strip, chunk):
    table = cosine_table()
    across = np.kron(np.eye(chunk // TILE), table)
    down = np.concatenate(
        [np.kron(np.eye(strip), table[0::2]), np.kron(np.eye(strip), table[1::2])], axis=0
    )
    row_high, row_low = split_bf16(down)
    col_high, col_low = split_bf16(across.T)
    row = jnp.concatenate([row_high, row_low], axis=1)
    inverse_row = jnp.asarray(down.T, jnp.float32).astype(jnp.bfloat16)
    inverse_col = jnp.asarray(across, jnp.float32).astype(jnp.bfloat16)
    return row, col_high, col_low, inverse_row, inverse_col


def flip(index, bits):
    bit = 1
    while bit <= bits:
        if bits & bit:
            index = index + bit - 2 * bit * ((index // bit) % 2)
        bit *= 2
    return index


def greet(axis, others):
    barrier = pltpu.get_barrier_semaphore()
    for other in others:
        pl.semaphore_signal(barrier, inc=1, device_id={axis: other}, device_id_type=MESH)
    pl.semaphore_wait(barrier, len(others))


def gather_kernel(size, block, out, send, recv, local):
    me = lax.axis_index("tensor")
    depth = size // 4
    z, x, core = me // 4, (me // 2) % 2, me % 2

    def slot(zz, xx, cc):
        return (zz * 2 + xx) * 2 + cc

    others = [flip(z, k) for k in range(1, depth)]
    side, twin = slot(z, 1 - x, core), slot(z, x, 1 - core)
    greet("tensor", [slot(zz, x, core) for zz in others] + [side, twin])
    own = pltpu.make_async_copy(block, out.at[me], local)
    own.start()
    copies = []

    def push(source, which, target):
        copy = pltpu.make_async_remote_copy(
            src_ref=source,
            dst_ref=out.at[which],
            send_sem=send.at[len(copies)],
            recv_sem=recv.at[which],
            device_id={"tensor": target},
            device_id_type=MESH,
        )
        copy.start()
        copies.append(copy)

    def arrive(which):
        pltpu.make_async_remote_copy(
            src_ref=block,
            dst_ref=out.at[which],
            send_sem=send.at[0],
            recv_sem=recv.at[which],
            device_id={"tensor": twin},
            device_id_type=MESH,
        ).wait_recv()

    push(block, me, side)
    for zz in others:
        push(block, me, slot(zz, x, core))
    push(block, me, twin)
    last = z
    for zz in others:
        which = slot(zz, x, core)
        arrive(which)
        push(out.at[which], which, side)
        push(out.at[which], which, twin)
        which = slot(last, 1 - x, core)
        arrive(which)
        push(out.at[which], which, twin)
        last = zz
    which = slot(last, 1 - x, core)
    arrive(which)
    push(out.at[which], which, twin)
    for zz in [z] + others:
        arrive(slot(zz, x, 1 - core))
        arrive(slot(zz, 1 - x, 1 - core))
    own.wait()
    for copy in copies:
        copy.wait_send()


def gather_blocks(block, size):
    return pl.pallas_call(
        functools.partial(gather_kernel, size),
        out_shape=jax.ShapeDtypeStruct((size,) + block.shape, block.dtype),
        in_specs=[VMEM],
        out_specs=VMEM,
        scratch_shapes=[
            pltpu.SemaphoreType.DMA((size,)),
            pltpu.SemaphoreType.DMA((size,)),
            pltpu.SemaphoreType.DMA,
        ],
        compiler_params=pltpu.CompilerParams(collective_id=0, has_side_effects=True),
        name="gather_blocks",
    )(block)


def exchange_kernel(replicas, values, out, send, recv):
    me = lax.axis_index("replica")
    greet("replica", [(me + k) % replicas for k in range(1, replicas)])
    copies = []
    for k in range(1, replicas):
        copy = pltpu.make_async_remote_copy(
            src_ref=values,
            dst_ref=out.at[k - 1],
            send_sem=send.at[k - 1],
            recv_sem=recv.at[k - 1],
            device_id={"replica": (me - k + replicas) % replicas},
            device_id_type=MESH,
        )
        copy.start()
        copies.append(copy)
    for copy in copies:
        copy.wait()


def exchange(values, replicas):
    return pl.pallas_call(
        functools.partial(exchange_kernel, replicas),
        out_shape=jax.ShapeDtypeStruct((replicas - 1,) + values.shape, values.dtype),
        in_specs=[VMEM],
        out_specs=VMEM,
        scratch_shapes=[
            pltpu.SemaphoreType.DMA((replicas - 1,)),
            pltpu.SemaphoreType.DMA((replicas - 1,)),
        ],
        compiler_params=pltpu.CompilerParams(collective_id=1, has_side_effects=True),
        name="exchange",
    )(values)


def scatter_kernel(size, parts, out, held, send, recv):
    me = lax.axis_index("tensor")
    greet("tensor", [(me + k) % size for k in range(1, size)])
    copies = []
    for k in range(1, size):
        target = (me + k) % size
        copy = pltpu.make_async_remote_copy(
            src_ref=parts.at[target],
            dst_ref=held.at[k - 1],
            send_sem=send.at[k - 1],
            recv_sem=recv.at[k - 1],
            device_id={"tensor": target},
            device_id_type=MESH,
        )
        copy.start()
        copies.append(copy)
    total = parts[me].astype(jnp.float32)
    for k in range(1, size):
        copies[k - 1].wait_recv()
        total = total + held[k - 1].astype(jnp.float32)
    out[...] = total.astype(out.dtype)
    for copy in copies:
        copy.wait_send()


def scatter_sum(parts):
    size = parts.shape[0]
    return pl.pallas_call(
        functools.partial(scatter_kernel, size),
        out_shape=jax.ShapeDtypeStruct(parts.shape[1:], parts.dtype),
        in_specs=[VMEM],
        out_specs=VMEM,
        scratch_shapes=[
            pltpu.VMEM((size - 1,) + parts.shape[1:], parts.dtype),
            pltpu.SemaphoreType.DMA((size - 1,)),
            pltpu.SemaphoreType.DMA((size - 1,)),
        ],
        compiler_params=pltpu.CompilerParams(collective_id=2, has_side_effects=True),
        name="scatter_sum",
    )(parts)


def dot(a, b):
    return jnp.dot(a, b, preferred_element_type=jnp.float32)


def contract(a, b, dim):
    return lax.dot_general(
        a, b, (((dim,), (dim,)), ((), ())), preferred_element_type=jnp.float32
    )


def lanes(shape):
    return lax.broadcasted_iota(jnp.int32, shape, 1) % TILE


def moment_kernel(
    chunk, hidden, grads, momentum, offsets, spread, row, col_high, col_low,
    inverse_row, inverse_col, kept, mine, sent,
):
    half = offsets.shape[0]
    place = lanes((half, chunk)).astype(jnp.float32)
    total = None
    for start in range(0, grads.shape[1], chunk):
        span = slice(start, start + chunk)
        moment = BETA_DECAY * momentum[0, :, span].astype(jnp.float32) + dot(
            hidden[...], grads[:, span]
        )
        rounded = moment.astype(jnp.bfloat16)
        mixed = dot(row[...], jnp.concatenate([rounded, rounded], axis=0)).astype(jnp.bfloat16)
        spectrum = dot(mixed, col_high[...]) + dot(mixed, col_low[...])
        offset = dot(offsets[...], spread[:, span])
        picked = jnp.where(
            offset == place,
            spectrum[:half],
            jnp.where(offset == place + TILE, spectrum[half:], 0.0),
        ).astype(jnp.bfloat16)
        values = contract(picked, spread[:, span], 1)
        total = values if total is None else total + values
        wide = dot(picked, inverse_col[...])
        odd = offset >= TILE
        pair = jnp.concatenate(
            [jnp.where(odd, 0.0, wide), jnp.where(odd, wide, 0.0)], axis=0
        ).astype(jnp.bfloat16)
        own = dot(inverse_row[...], pair)
        kept[0, :, span] = (moment - own).astype(jnp.bfloat16)
        mine[:, span] = own.astype(jnp.bfloat16)
    sent[...] = total.astype(jnp.bfloat16)


def whole_block(array):
    return pl.BlockSpec(array.shape, lambda i: (0,) * array.ndim)


def moment_pass(hidden, grads, momentum, offsets, spread, mats, strip, chunk):
    rows, breadth = momentum.shape[1:]
    tall = strip * TILE
    half = tall // 2
    columns = spread.shape[0]
    row, col_high, col_low, inverse_row, inverse_col = mats
    return pl.pallas_call(
        functools.partial(moment_kernel, chunk),
        grid=(rows // tall,),
        out_shape=(
            jax.ShapeDtypeStruct((1, rows, breadth), jnp.bfloat16),
            jax.ShapeDtypeStruct((rows, breadth), jnp.bfloat16),
            jax.ShapeDtypeStruct((rows // 2, columns), jnp.bfloat16),
        ),
        in_specs=[
            pl.BlockSpec((tall, hidden.shape[1]), lambda i: (i, 0)),
            whole_block(grads),
            pl.BlockSpec((1, tall, breadth), lambda i: (0, i, 0)),
            pl.BlockSpec((half, columns), lambda i: (i, 0)),
            whole_block(spread),
            whole_block(row),
            whole_block(col_high),
            whole_block(col_low),
            whole_block(inverse_row),
            whole_block(inverse_col),
        ],
        out_specs=(
            pl.BlockSpec((1, tall, breadth), lambda i: (0, i, 0)),
            pl.BlockSpec((tall, breadth), lambda i: (i, 0)),
            pl.BlockSpec((half, columns), lambda i: (i, 0)),
        ),
        name="moment_pass",
    )(hidden, grads, momentum, offsets, spread, row, col_high, col_low, inverse_row, inverse_col)


def output_kernel(
    chunk, replicas, hidden, down, mine, values, offsets, spread, inverse_row, inverse_col,
    out, total,
):
    step = pl.program_id(0)
    half = offsets.shape[1]
    place = lanes((half, chunk)).astype(jnp.float32)

    @pl.when(step == 0)
    def _():
        total[...] = jnp.zeros_like(total)

    for start in range(0, down.shape[1], chunk):
        span = slice(start, start + chunk)
        even = odd = 0.0
        for k in range(replicas - 1):
            offset = dot(offsets[k], spread[:, span])
            value = dot(values[k], spread[:, span])
            even = even + jnp.where(offset == place, value, 0.0)
            odd = odd + jnp.where(offset == place + TILE, value, 0.0)
        placed = jnp.concatenate([even, odd], axis=0).astype(jnp.bfloat16)
        wide = dot(placed, inverse_col[...]).astype(jnp.bfloat16)
        update = mine[:, span].astype(jnp.float32) + dot(inverse_row[...], wide)
        new = down[:, span].astype(jnp.float32) - (STEP_RATE / replicas) * update
        total[:, span] += contract(hidden[...], new.astype(jnp.bfloat16), 0)

    @pl.when(step == pl.num_programs(0) - 1)
    def _():
        out[...] = total[...].astype(out.dtype)


def output_pass(hidden, down, mine, values, offsets, spread, mats, strip, chunk, replicas):
    rows, breadth = down.shape
    tall = strip * TILE
    half = tall // 2
    columns = spread.shape[0]
    count = hidden.shape[1]
    inverse_row, inverse_col = mats[3:]
    return pl.pallas_call(
        functools.partial(output_kernel, chunk, replicas),
        grid=(rows // tall,),
        out_shape=jax.ShapeDtypeStruct((count, breadth), jnp.bfloat16),
        in_specs=[
            pl.BlockSpec((tall, count), lambda i: (i, 0)),
            pl.BlockSpec((tall, breadth), lambda i: (i, 0)),
            pl.BlockSpec((tall, breadth), lambda i: (i, 0)),
            pl.BlockSpec((replicas - 1, half, columns), lambda i: (0, i, 0)),
            pl.BlockSpec((replicas - 1, half, columns), lambda i: (0, i, 0)),
            whole_block(spread),
            whole_block(inverse_row),
            whole_block(inverse_col),
        ],
        out_specs=pl.BlockSpec((count, breadth), lambda i: (0, 0)),
        scratch_shapes=[pltpu.VMEM((count, breadth), jnp.float32)],
        name="output_pass",
    )(hidden, down, mine, values, offsets, spread, inverse_row, inverse_col)


def on_device(
    tokens, next_tokens, cotangent, gate_weight, up_weight, down_weight, momentum, indices
):
    size = lax.axis_size("tensor")
    replicas = lax.axis_size("replica")
    replica = lax.axis_index("replica")
    count, share = tokens.shape
    nexts = next_tokens.shape[0]
    breadth = share * size
    tile_rows, tile_cols, keep = indices.shape[1:]
    strip = next(n for n in (4, 2, 1) if tile_rows % n == 0)
    chunk = next(n for n in (256, 128) if breadth % n == 0)

    turned = next_tokens.T
    block = jnp.concatenate(
        [
            cotangent.T,
            tokens.T,
            jnp.concatenate([turned[: share // 2], turned[share // 2 :]], axis=1),
        ],
        axis=0,
    )
    gathered = gather_blocks(block, size)
    grads = gathered[:, :share].reshape(breadth, count).T
    features = gathered[:, share : 2 * share].reshape(breadth, count)
    tail = gathered[:, 2 * share :]
    next_features = jnp.concatenate([tail[:, :, :nexts], tail[:, :, nexts:]], axis=1)
    features = jnp.concatenate([features, next_features.reshape(breadth, nexts)], axis=1)
    gate = contract(gate_weight, features, 0)
    upper = contract(up_weight, features, 0)
    hidden = (jax.nn.silu(gate) * upper).astype(jnp.bfloat16)

    stride = TILE * TILE // keep
    offsets = indices - jnp.arange(keep, dtype=jnp.int32) * stride
    offsets = jnp.swapaxes(offsets.astype(jnp.bfloat16), 2, 3)
    offsets = offsets.reshape(replicas, tile_rows * keep, tile_cols)
    spread = jnp.asarray(np.kron(np.eye(tile_cols), np.ones((1, TILE))), jnp.bfloat16)
    mats = tables(strip, chunk)
    own_offsets = lax.dynamic_index_in_dim(offsets, replica, 0, keepdims=False)
    kept, mine, sent = moment_pass(
        hidden[:, :count], grads, momentum, own_offsets, spread, mats, strip, chunk
    )
    values = exchange(sent, replicas)
    other_offsets = jnp.stack(
        [
            lax.dynamic_index_in_dim(offsets, (replica + k) % replicas, 0, keepdims=False)
            for k in range(1, replicas)
        ]
    )
    partial = output_pass(
        hidden[:, count:], down_weight, mine, values, other_offsets, spread, mats, strip, chunk,
        replicas,
    )
    output = scatter_sum(partial.reshape(size, nexts // size, breadth))
    return (output, kept)


def solution(mesh):
    return jax.shard_map(
        on_device,
        mesh=mesh,
        in_specs=(
            P("replica", "tensor"),
            P("replica", "tensor"),
            P("replica", "tensor"),
            P(None, "tensor"),
            P(None, "tensor"),
            P("tensor", None),
            P("replica", "tensor", None),
            P(None, "tensor", None, None),
        ),
        out_specs=(P(("replica", "tensor"), None), P("replica", "tensor", None)),
        check_vma=False,
    )
```

time: 508 us -> 134 us (0.26); the launches traced: 497 us -> 133 us
  matrix products: 175 us -> 6.28 us
  local copies, waits for them, and re-layouts: 127 us -> 9.84 us
  Pallas kernels: 0 us -> 114 us
  waiting for transfers between devices: 75.7 us -> 0 us
  blocking collectives: 71.2 us -> 0 us
  other arithmetic: 33.1 us -> 2.79 us
  between operations: 15.3 us -> 0.75 us
    dot_general x10 -> x2, matrix products: 175 us -> 6.28 us  [contract(): lax.dot_general(a, b, (((dim,), (dim,)), ((), ())), preferred_element_typ...]
    pallas_call x0 -> x5, Pallas kernels: none -> 114 us  [the longest x1 39.1 us: moment_pass(): pl.pallas_call(functools.partial(moment_kernel, chunk), grid=(rows // tal...]
    unnamed x3 -> x0, waiting for transfers between devices: 75.7 us -> none
    all_gather x4 -> x0, blocking collectives: 71.2 us -> none  [the longest x1 25.3 us: on_device(): lax.all_gather(tokens, 'tensor', axis=1, tiled=True)]
    mul x8 -> x0, local copies, waits for them, and re-layouts: 37.6 us -> none  [the longest x2 21 us: on_device(): STEP_RATE * update]
    reshape x3 -> x2, local copies, waits for them, and re-layouts: 38.7 us -> 2.85 us  [the longest x1 1.77 us: on_device(): output = scatter_sum(partial.reshape(size, nexts // size, breadth))]
    transpose x1 -> x0, local copies, waits for them, and re-layouts: 20.5 us -> none  [inverse_tiles(): jnp.einsum('ak,xyab,bl->xkyl', table, blocks, table, precision=lax.Precis...]
    eq x10 -> x0, local copies, waits for them, and re-layouts: 19.7 us -> none  [one_hot_slots(): return (offset[..., None] == slots).astype(jnp.float32)]
  transfers between devices with their start and end apart: 2 -> 0, of which waited for: 1 -> 0; matrix products, arithmetic and copies ran while one was open for 25% -> 0% of each run, Pallas kernels for 0% -> 0%
where the time goes in v1:
time: 134 us; the launch traced here: 133 us
  Pallas kernels  114 us (85%)
  local copies, waits for them, and re-layouts  9.84 us (7%)
  matrix products  6.28 us (5%)
  other arithmetic  2.79 us (2%)
    pallas_call x1, Pallas kernels, moment_pass(): pl.pallas_call(functools.partial(moment_kernel, chunk), grid=(rows // tal...  39.1 us
    pallas_call x1, Pallas kernels, output_pass(): pl.pallas_call(functools.partial(output_kernel, chunk, replicas), grid=(r...  34.3 us
    pallas_call x1, Pallas kernels, gather_blocks(): pl.pallas_call(functools.partial(gather_kernel, size), out_shape=jax.Shap...  22.5 us
    pallas_call x1, Pallas kernels, scatter_sum(): pl.pallas_call(functools.partial(scatter_kernel, size), out_shape=jax.Sha...  10.8 us
    pallas_call x1, Pallas kernels, exchange(): pl.pallas_call(functools.partial(exchange_kernel, replicas), out_shape=ja...  7.01 us
    dot_general x2, matrix products, contract(): lax.dot_general(a, b, (((dim,), (dim,)), ((), ())), preferred_element_typ...  6.28 us

profile of v1, /device:TPU:0, one launch (start us, length us, event | category | flops | bytes accessed | tf_op | source)
XLA Modules:
  0.0 133.2 jit_solution(10212725978524731595)
XLA Ops:
  0.7 0.9 copy.21
  1.5 1.5 %maximum_maximum_fusion.block = bf16[400,128]{1,0:T(8,128)(2,1)} fusion(bf16[80,64]{1,0:T(8,128)(2,1)S(1)} %get-tuple-element.15, bf16[80,64]{1,0:T(8,128)(2,1)S(1)} %get-tuple-element.14, bf16[160,128]{1,0:T(8,128)(2,1)} %bitcast.30, bf16[160,128]{1,0:T(8,128)(2,1)} %bitcast.31), kind=kLoop, calls=%fused_computation.8 | loop fusion | flops 409600 | bytes 204800 | tf_op jit(solution)/shard_map/concatenate | solution.py:374
  3.1 1.1 subtract_convert_fusion
  4.2 0.7 constant_dynamic-slice_fusion
  4.9 22.5 %gather_blocks.1 = bf16[16,400,128]{2,1,0:T(8,128)(2,1)} custom-call(bf16[400,128]{1,0:T(8,128)(2,1)} %maximum_maximum_fusion.block), custom_call_target="tpu_custom_call" | custom-call | tf_op jit(solution)/shard_map/gather_blocks/pallas_call | solution.py:124
  27.4 1.2 fusion.5
  28.6 1.4 %fusion.4 = (bf16[16,160,128]{2,1,0:T(8,128)(2,1)S(1)}, bf16[16,160,128]{2,1,0:T(8,128)(2,1)S(1)}) fusion(bf16[16,400,128]{2,1,0:T(8,128)(2,1)} %gather_blocks.1), kind=kLoop, calls=%fused_computation.13 | loop fusion | bytes 2621440 | tf_op jit(solution)/shard_map/slice | solution.py:383
  30.0 1.1 copy.24
  31.1 0.0 slice-start
  31.1 0.1 pad_maximum_fusion.3
  31.2 0.0 slice-start.1
  31.2 4.4 %convolution_bitcast_fusion.1 = f32[896,192]{1,0:T(8,128)S(1)} fusion(bf16[2560,896]{1,0:T(8,128)(2,1)} %param.18, bf16[2560,64]{1,0:T(8,128)(2,1)S(1)} %bitcast.27, bf16[2560,128]{1,0:T(8,128)(2,1)S(1)} %bitcast.25), kind=kOutput, calls=%fused_computation.2 | convolution fusion | flops 882769920 | bytes 6258688 | tf_op jit(solution)/shard_map/dot_general | solution.py:220
  35.6 0.0 slice-done
  35.6 0.0 slice-done.1
  35.6 1.9 %fusion.1 = bf16[896,192]{1,0:T(8,128)(2,1)S(1)} fusion(bf16[2560,896]{1,0:T(8,128)(2,1)S(1)} %bitcast.33, f32[896,192]{1,0:T(8,128)S(1)} %convolution_bitcast_fusion.1, bf16[2560,64]{1,0:T(8,128)(2,1)S(1)} %bitcast.28, bf16[2560,128]{1,0:T(8,128)(2,1)S(1)} %bitcast.26), kind=kOutput, calls=%fused_computation.4 | convolution fusion | flops 883802112 | bytes 6602752 | tf_op jit(solution)/shard_map/dot_general | solution.py:220
  37.6 0.7 slice.38.hidden
  38.3 0.7 slice.37.hidden
  39.0 39.1 %moment_pass.1 = (bf16[1,896,2560]{2,1,0:T(8,128)(2,1)}, bf16[896,2560]{1,0:T(8,128)(2,1)}, bf16[448,40]{1,0:T(8,128)(2,1)}) custom-call(bf16[896,128]{1,0:T(8,128)(2,1)} %slice.38.hidden, bf16[128,2560]{1,0:T(8,128)(2,1)} %bitcast.22, bf16[1,896,2560]{2,1,0:T(8,128)(2,1)} %momentum.1, bf16[448,40]{1,0:T(8,128)(2,1)} %get-tuple-element.13.offsets, ...), custom_call_target="tpu_custom_call" | custom-call | tf_op jit(solution)/shard_map/moment_pass/pallas_call | solution.py:273
  78.1 7.0 %exchange.1.values = bf16[1,448,40]{2,1,0:T(8,128)(2,1)} custom-call(bf16[448,40]{1,0:T(8,128)(2,1)} %get-tuple-element.6.values), custom_call_target="tpu_custom_call" | custom-call | tf_op jit(solution)/shard_map/exchange/pallas_call | solution.py:159
  85.1 34.3 %output_pass.1 = bf16[64,2560]{1,0:T(8,128)(2,1)} custom-call(bf16[896,64]{1,0:T(8,128)(2,1)} %slice.37.hidden, bf16[896,2560]{1,0:T(8,128)(2,1)} %down.1, bf16[896,2560]{1,0:T(8,128)(2,1)} %get-tuple-element.5.mine, bf16[1,448,40]{2,1,0:T(8,128)(2,1)} %exchange.1.values, bf16[1,448,40]{2,1,0:T(8,128)(2,1)} %get-tuple-element.12.offsets, ...), custom_call_target="tpu_custom_call" | custom-call | tf_op jit(solution)/shard_map/output_pass/pallas_call | solution.py:340
  119.3 1.8 %reshape.27.parts = bf16[16,4,2560]{2,1,0:T(4,128)(2,1)} reshape(bf16[64,2560]{1,0:T(8,128)(2,1)} %output_pass.1) | data formatting | bytes 655360 | tf_op jit(solution)/shard_map/reshape | solution.py:413
  121.1 10.8 %scatter_sum.1 = bf16[4,2560]{1,0:T(4,128)(2,1)} custom-call(bf16[16,4,2560]{2,1,0:T(4,128)(2,1)} %reshape.27.parts), custom_call_target="tpu_custom_call" | custom-call | tf_op jit(solution)/shard_map/scatter_sum/pallas_call | solution.py:200
  131.9 1.3 %copy.28 = bf16[4,2560]{1,0:T(4,128)(2,1)} copy(bf16[4,2560]{1,0:T(4,128)(2,1)} %scatter_sum.1) | data formatting | bytes 40960
  (3 shorter events, 0.0 us)
Async XLA Ops:
  31.1 4.5 %slice-start = ((s8[4587520]{0:T(1024)(128)(4,1)}), s8[4194304]{0:T(1024)(128)(4,1)S(1)}, s32[]{:S(2)}) async-start(s8[4587520]{0:T(1024)(128)(4,1)} %bitcast.32), calls=%async_computation | async-start | bytes 8388608
  31.2 4.4 %slice-start.1 = ((s8[4587520]{0:T(1024)(128)(4,1)}), s8[393216]{0:T(1024)(128)(4,1)S(1)}, s32[]{:S(2)}) async-start(s8[4587520]{0:T(1024)(128)(4,1)} %bitcast.32), calls=%async_computation.1 | async-start | bytes 786432

commit v2 on v1

--- a/solution.py
+++ b/solution.py
@@ -99,19 +99,15 @@
     for zz in others:
         push(block, me, slot(zz, x, core))
     push(block, me, twin)
-    last = z
     for zz in others:
         which = slot(zz, x, core)
         arrive(which)
         push(out.at[which], which, side)
         push(out.at[which], which, twin)
-        which = slot(last, 1 - x, core)
+    for zz in [z] + others:
+        which = slot(zz, 1 - x, core)
         arrive(which)
         push(out.at[which], which, twin)
-        last = zz
-    which = slot(last, 1 - x, core)
-    arrive(which)
-    push(out.at[which], which, twin)
     for zz in [z] + others:
         arrive(slot(zz, x, 1 - core))
         arrive(slot(zz, 1 - x, 1 - core))
@@ -226,50 +222,70 @@
     return lax.broadcasted_iota(jnp.int32, shape, 1) % TILE
 
 
+def strip_offsets(indices, which):
+    strip, columns, keep = indices.shape[1:]
+    first = lax.broadcasted_iota(jnp.int32, (columns, keep), 1) * (TILE * TILE // keep)
+    listed = [
+        (indices[which, n] - first).astype(jnp.float32).astype(jnp.bfloat16) for n in range(strip)
+    ]
+    return jnp.concatenate(listed, axis=1)
+
+
 def moment_kernel(
-    chunk, hidden, grads, momentum, offsets, spread, row, col_high, col_low,
+    chunk, hidden, grads, momentum, indices, spread, gather, row, col_high, col_low,
     inverse_row, inverse_col, kept, mine, sent,
+    moment, mixed, offset, picked, stacked, pair,
 ):
-    half = offsets.shape[0]
+    tall, breadth = moment.shape
+    half = tall // 2
+    spans = [slice(start, start + chunk) for start in range(0, breadth, chunk)]
+    own_offsets = strip_offsets(indices, lax.axis_index("replica"))
+    for span in spans:
+        offset[:, span] = contract(own_offsets, spread[:, span], 0)
+    for span in spans:
+        moment[:, span] = BETA_DECAY * momentum[0, :, span].astype(jnp.float32) + contract(
+            hidden[...], grads[span, :], 1
+        )
+    for k, span in enumerate(spans):
+        rounded = moment[:, span].astype(jnp.bfloat16)
+        mixed[k * tall : (k + 1) * tall] = dot(
+            row[...], jnp.concatenate([rounded, rounded], axis=0)
+        ).astype(jnp.bfloat16)
     place = lanes((half, chunk)).astype(jnp.float32)
-    total = None
-    for start in range(0, grads.shape[1], chunk):
-        span = slice(start, start + chunk)
-        moment = BETA_DECAY * momentum[0, :, span].astype(jnp.float32) + dot(
-            hidden[...], grads[:, span]
-        )
-        rounded = moment.astype(jnp.bfloat16)
-        mixed = dot(row[...], jnp.concatenate([rounded, rounded], axis=0)).astype(jnp.bfloat16)
-        spectrum = dot(mixed, col_high[...]) + dot(mixed, col_low[...])
-        offset = dot(offsets[...], spread[:, span])
-        picked = jnp.where(
-            offset == place,
+    for k, span in enumerate(spans):
+        part = mixed[k * tall : (k + 1) * tall]
+        spectrum = dot(part, col_high[...]) + dot(part, col_low[...])
+        where = offset[:, span]
+        values = jnp.where(
+            where == place,
             spectrum[:half],
-            jnp.where(offset == place + TILE, spectrum[half:], 0.0),
+            jnp.where(where == place + TILE, spectrum[half:], 0.0),
         ).astype(jnp.bfloat16)
-        values = contract(picked, spread[:, span], 1)
-        total = values if total is None else total + values
-        wide = dot(picked, inverse_col[...])
-        odd = offset >= TILE
-        pair = jnp.concatenate(
-            [jnp.where(odd, 0.0, wide), jnp.where(odd, wide, 0.0)], axis=0
-        ).astype(jnp.bfloat16)
-        own = dot(inverse_row[...], pair)
-        kept[0, :, span] = (moment - own).astype(jnp.bfloat16)
+        picked[:, span] = values
+        stacked[k * half : (k + 1) * half] = values
+    sent[...] = dot(picked[...], gather[...]).astype(jnp.bfloat16)
+    for k, span in enumerate(spans):
+        wide = dot(stacked[k * half : (k + 1) * half], inverse_col[...])
+        odd = offset[:, span] >= TILE
+        pair[:half, span] = jnp.where(odd, 0.0, wide).astype(jnp.bfloat16)
+        pair[half:, span] = jnp.where(odd, wide, 0.0).astype(jnp.bfloat16)
+    for span in spans:
+        own = dot(inverse_row[...], pair[:, span])
+        kept[0, :, span] = (moment[:, span] - own).astype(jnp.bfloat16)
         mine[:, span] = own.astype(jnp.bfloat16)
-    sent[...] = total.astype(jnp.bfloat16)
 
 
 def whole_block(array):
     return pl.BlockSpec(array.shape, lambda i: (0,) * array.ndim)
 
 
-def moment_pass(hidden, grads, momentum, offsets, spread, mats, strip, chunk):
+def moment_pass(hidden, grads, momentum, indices, spread, mats, strip, chunk):
     rows, breadth = momentum.shape[1:]
     tall = strip * TILE
-    half = tall // 2
-    columns = spread.shape[0]
+    replicas, _, columns, keep = indices.shape
+    half = strip * keep
     row, col_high, col_low, inverse_row, inverse_col = mats
+    gather = spread.T
     return pl.pallas_call(
         functools.partial(moment_kernel, chunk),
         grid=(rows // tall,),
@@ -282,8 +298,9 @@
             pl.BlockSpec((tall, hidden.shape[1]), lambda i: (i, 0)),
             whole_block(grads),
             pl.BlockSpec((1, tall, breadth), lambda i: (0, i, 0)),
-            pl.BlockSpec((half, columns), lambda i: (i, 0)),
+            pl.BlockSpec((replicas, strip, columns, keep), lambda i: (0, i, 0, 0)),
             whole_block(spread),
+            whole_block(gather),
             whole_block(row),
             whole_block(col_high),
             whole_block(col_low),
@@ -295,66 +312,98 @@
             pl.BlockSpec((tall, breadth), lambda i: (i, 0)),
             pl.BlockSpec((half, columns), lambda i: (i, 0)),
         ),
+        scratch_shapes=[
+            pltpu.VMEM((tall, breadth), jnp.float32),
+            pltpu.VMEM((tall * (breadth // chunk), chunk), jnp.bfloat16),
+            pltpu.VMEM((half, breadth), jnp.float32),
+            pltpu.VMEM((half, breadth), jnp.bfloat16),
+            pltpu.VMEM((half * (breadth // chunk), chunk), jnp.bfloat16),
+            pltpu.VMEM((tall, breadth), jnp.bfloat16),
+        ],
         name="moment_pass",
-    )(hidden, grads, momentum, offsets, spread, row, col_high, col_low, inverse_row, inverse_col)
+    )(
+        hidden, grads, momentum, indices, spread, gather, row, col_high, col_low, inverse_row,
+        inverse_col,
+    )
 
 
 def output_kernel(
-    chunk, replicas, hidden, down, mine, values, offsets, spread, inverse_row, inverse_col,
-    out, total,
+    chunk, hidden, down, mine, values, indices, spread, inverse_row, inverse_col,
+    out, total, placed, wide, new,
 ):
     step = pl.program_id(0)
-    half = offsets.shape[1]
-    place = lanes((half, chunk)).astype(jnp.float32)
+    replicas, strip, _, keep = indices.shape
+    half = strip * keep
+    tall, breadth = new.shape
+    spans = [slice(start, start + chunk) for start in range(0, breadth, chunk)]
+    replica = lax.axis_index("replica")
 
     @pl.when(step == 0)
     def _():
         total[...] = jnp.zeros_like(total)
 
-    for start in range(0, down.shape[1], chunk):
-        span = slice(start, start + chunk)
+    place = lanes((half, chunk)).astype(jnp.float32)
+    listed = [
+        strip_offsets(indices, (replica + k) % replicas) for k in range(1, replicas)
+    ]
+    for n, span in enumerate(spans):
         even = odd = 0.0
         for k in range(replicas - 1):
-            offset = dot(offsets[k], spread[:, span])
+            offset = contract(listed[k], spread[:, span], 0)
             value = dot(values[k], spread[:, span])
             even = even + jnp.where(offset == place, value, 0.0)
             odd = odd + jnp.where(offset == place + TILE, value, 0.0)
-        placed = jnp.concatenate([even, odd], axis=0).astype(jnp.bfloat16)
-        wide = dot(placed, inverse_col[...]).astype(jnp.bfloat16)
-        update = mine[:, span].astype(jnp.float32) + dot(inverse_row[...], wide)
-        new = down[:, span].astype(jnp.float32) - (STEP_RATE / replicas) * update
-        total[:, span] += contract(hidden[...], new.astype(jnp.bfloat16), 0)
+        placed[n * tall : n * tall + half] = even.astype(jnp.bfloat16)
+        placed[n * tall + half : (n + 1) * tall] = odd.astype(jnp.bfloat16)
+    for n, span in enumerate(spans):
+        wide[:, span] = dot(placed[n * tall : (n + 1) * tall], inverse_col[...]).astype(
+            jnp.bfloat16
+        )
+    for span in spans:
+        update = mine[:, span].astype(jnp.float32) + dot(inverse_row[...], wide[:, span])
+        new[:, span] = (
+            down[:, span].astype(jnp.float32) - (STEP_RATE / replicas) * update
+        ).astype(jnp.bfloat16)
+    for span in spans:
+        total[:, span] += contract(hidden[...], new[:, span], 0)
 
     @pl.when(step == pl.num_programs(0) - 1)
     def _():
-        out[...] = total[...].astype(out.dtype)
-
-
-def output_pass(hidden, down, mine, values, offsets, spread, mats, strip, chunk, replicas):
+        size, rows, _ = out.shape
+        for n in range(size):
+            out[n] = total[n * rows : (n + 1) * rows].astype(out.dtype)
+
+
+def output_pass(hidden, down, mine, values, indices, spread, mats, strip, chunk, size):
     rows, breadth = down.shape
     tall = strip * TILE
-    half = tall // 2
-    columns = spread.shape[0]
+    replicas, _, columns, keep = indices.shape
+    half = strip * keep
     count = hidden.shape[1]
     inverse_row, inverse_col = mats[3:]
     return pl.pallas_call(
-        functools.partial(output_kernel, chunk, replicas),
+        functools.partial(output_kernel, chunk),
         grid=(rows // tall,),
-        out_shape=jax.ShapeDtypeStruct((count, breadth), jnp.bfloat16),
+        out_shape=jax.ShapeDtypeStruct((size, count // size, breadth), jnp.bfloat16),
         in_specs=[
             pl.BlockSpec((tall, count), lambda i: (i, 0)),
             pl.BlockSpec((tall, breadth), lambda i: (i, 0)),
             pl.BlockSpec((tall, breadth), lambda i: (i, 0)),
             pl.BlockSpec((replicas - 1, half, columns), lambda i: (0, i, 0)),
-            pl.BlockSpec((replicas - 1, half, columns), lambda i: (0, i, 0)),
+            pl.BlockSpec((replicas, strip, columns, keep), lambda i: (0, i, 0, 0)),
             whole_block(spread),
             whole_block(inverse_row),
             whole_block(inverse_col),
         ],
-        out_specs=pl.BlockSpec((count, breadth), lambda i: (0, 0)),
-        scratch_shapes=[pltpu.VMEM((count, breadth), jnp.float32)],
+        out_specs=pl.BlockSpec((size, count // size, breadth), lambda i: (0, 0, 0)),
+        scratch_shapes=[
+            pltpu.VMEM((count, breadth), jnp.float32),
+            pltpu.VMEM((tall * (breadth // chunk), chunk), jnp.bfloat16),
+            pltpu.VMEM((tall, breadth), jnp.bfloat16),
+            pltpu.VMEM((tall, breadth), jnp.bfloat16),
+        ],
         name="output_pass",
-    )(hidden, down, mine, values, offsets, spread, inverse_row, inverse_col)
+    )(hidden, down, mine, values, indices, spread, inverse_row, inverse_col)
 
 
 def on_device(
@@ -362,7 +411,6 @@
 ):
     size = lax.axis_size("tensor")
     replicas = lax.axis_size("replica")
-    replica = lax.axis_index("replica")
     count, share = tokens.shape
     nexts = next_tokens.shape[0]
     breadth = share * size
@@ -380,7 +428,7 @@
         axis=0,
     )
     gathered = gather_blocks(block, size)
-    grads = gathered[:, :share].reshape(breadth, count).T
+    grads = gathered[:, :share].reshape(breadth, count)
     features = gathered[:, share : 2 * share].reshape(breadth, count)
     tail = gathered[:, 2 * share :]
     next_features = jnp.concatenate([tail[:, :, :nexts], tail[:, :, nexts:]], axis=1)
@@ -389,28 +437,16 @@
     upper = contract(up_weight, features, 0)
     hidden = (jax.nn.silu(gate) * upper).astype(jnp.bfloat16)
 
-    stride = TILE * TILE // keep
-    offsets = indices - jnp.arange(keep, dtype=jnp.int32) * stride
-    offsets = jnp.swapaxes(offsets.astype(jnp.bfloat16), 2, 3)
-    offsets = offsets.reshape(replicas, tile_rows * keep, tile_cols)
     spread = jnp.asarray(np.kron(np.eye(tile_cols), np.ones((1, TILE))), jnp.bfloat16)
     mats = tables(strip, chunk)
-    own_offsets = lax.dynamic_index_in_dim(offsets, replica, 0, keepdims=False)
     kept, mine, sent = moment_pass(
-        hidden[:, :count], grads, momentum, own_offsets, spread, mats, strip, chunk
+        hidden[:, :count], grads, momentum, indices, spread, mats, strip, chunk
     )
     values = exchange(sent, replicas)
-    other_offsets = jnp.stack(
-        [
-            lax.dynamic_index_in_dim(offsets, (replica + k) % replicas, 0, keepdims=False)
-            for k in range(1, replicas)
-        ]
-    )
     partial = output_pass(
-        hidden[:, count:], down_weight, mine, values, other_offsets, spread, mats, strip, chunk,
-        replicas,
-    )
-    output = scatter_sum(partial.reshape(size, nexts // size, breadth))
+        hidden[:, count:], down_weight, mine, values, indices, spread, mats, strip, chunk, size
+    )
+    output = scatter_sum(partial)
     return (output, kept)
 
 

time: 134 us -> 82.6 us (0.62)
  Pallas kernels: 114 us -> 66 us
  matrix products: 6.28 us -> 3.83 us
    pallas_call x1, Pallas kernels: 34.3 us -> 10.3 us  [output_pass(): pl.pallas_call(functools.partial(output_kernel, chunk), grid=(rows // tal...]
    pallas_call x1, Pallas kernels: 39.1 us -> 15.4 us  [moment_pass(): pl.pallas_call(functools.partial(moment_kernel, chunk), grid=(rows // tal...]
    reshape x2 -> x0, local copies, waits for them, and re-layouts: 2.85 us -> none  [the longest x1 1.77 us: on_device(): output = scatter_sum(partial.reshape(size, nexts // size, breadth))]
    dot_general x2, matrix products: 6.28 us -> 3.83 us  [contract(): lax.dot_general(a, b, (((dim,), (dim,)), ((), ())), preferred_element_typ...]
    unnamed x6 -> x9, local copies, waits for them, and re-layouts: 2.22 us -> 4.52 us
where the time goes in v2:
time: 82.6 us; the launch traced here: 81.9 us
  Pallas kernels  66 us (80%)
  local copies, waits for them, and re-layouts  9.7 us (12%)
  matrix products  3.83 us (5%)
  other arithmetic  1.66 us (2%)
    pallas_call x1, Pallas kernels, gather_blocks(): pl.pallas_call(functools.partial(gather_kernel, size), out_shape=jax.Shap...  22.5 us
    pallas_call x1, Pallas kernels, moment_pass(): pl.pallas_call(functools.partial(moment_kernel, chunk), grid=(rows // tal...  15.4 us
    pallas_call x1, Pallas kernels, scatter_sum(): pl.pallas_call(functools.partial(scatter_kernel, size), out_shape=jax.Sha...  10.8 us
    pallas_call x1, Pallas kernels, output_pass(): pl.pallas_call(functools.partial(output_kernel, chunk), grid=(rows // tal...  10.3 us
    pallas_call x1, Pallas kernels, exchange(): pl.pallas_call(functools.partial(exchange_kernel, replicas), out_shape=ja...  7.03 us
    unnamed x9, local copies, waits for them, and re-layouts  4.52 us
    dot_general x2, matrix products, contract(): lax.dot_general(a, b, (((dim,), (dim,)), ((), ())), preferred_element_typ...  3.83 us
    slice x1, local copies, waits for them, and re-layouts, on_device(): grads = gathered[:, :share].reshape(breadth, count)  2.38 us

profile of v2, /device:TPU:0, one launch (start us, length us, event | category | flops | bytes accessed | tf_op | source)
XLA Modules:
  0.0 81.9 jit_solution(13726702864296086724)
XLA Ops:
  0.6 0.9 %copy.17 = bf16[64,160]{0,1:T(8,128)(2,1)S(1)} copy(bf16[64,160]{1,0:T(8,128)(2,1)} %param.16) | data formatting | bytes 40960 | tf_op args[1]
  1.5 1.5 %maximum_maximum_fusion.block = bf16[400,128]{1,0:T(8,128)(2,1)} fusion(bf16[80,64]{1,0:T(8,128)(2,1)S(1)} %get-tuple-element.13, bf16[80,64]{1,0:T(8,128)(2,1)S(1)} %get-tuple-element.12, bf16[160,128]{1,0:T(8,128)(2,1)} %bitcast.22, bf16[160,128]{1,0:T(8,128)(2,1)} %bitcast.23), kind=kLoop, calls=%fused_computation.6 | loop fusion | flops 409600 | bytes 204800 | tf_op jit(solution)/shard_map/concatenate | solution.py:422
  3.0 2.1 %copy.20.indices = s32[2,14,40,32]{3,2,1,0:T(8,128)} copy(s32[2,14,40,32]{2,3,1,0:T(8,128)} %param.22) | data formatting | bytes 286720 | tf_op args[7]
  5.1 22.5 %gather_blocks.1 = bf16[16,400,128]{2,1,0:T(8,128)(2,1)} custom-call(bf16[400,128]{1,0:T(8,128)(2,1)} %maximum_maximum_fusion.block), custom_call_target="tpu_custom_call" | custom-call | tf_op jit(solution)/shard_map/gather_blocks/pallas_call | solution.py:120
  27.6 0.0 copy-start
  27.6 1.4 %fusion.5 = (bf16[16,80,64]{2,1,0:T(8,128)(2,1)S(1)}, bf16[16,80,64]{2,1,0:T(8,128)(2,1)S(1)}) fusion(bf16[16,400,128]{2,1,0:T(8,128)(2,1)} %gather_blocks.1), kind=kLoop, calls=%fused_computation.10 | loop fusion | bytes 655360 | tf_op jit(solution)/shard_map/slice | solution.py:434
  29.0 2.4 %fusion.4 = (bf16[16,160,128]{2,1,0:T(8,128)(2,1)}, bf16[16,160,128]{2,1,0:T(8,128)(2,1)S(1)}) fusion(bf16[16,400,128]{2,1,0:T(8,128)(2,1)} %gather_blocks.1), kind=kLoop, calls=%fused_computation.9 | loop fusion | bytes 2621440 | tf_op jit(solution)/shard_map/slice | solution.py:431
  31.4 0.0 slice-start
  31.4 0.1 pad_maximum_fusion.3
  31.5 0.0 copy-done
  31.5 0.0 slice-start.1
  31.5 1.9 %convolution_bitcast_fusion.1 = f32[896,192]{1,0:T(8,128)S(1)} fusion(bf16[2560,896]{1,0:T(8,128)(2,1)S(1)} %copy-done, bf16[2560,64]{1,0:T(8,128)(2,1)S(1)} %bitcast.19, bf16[2560,128]{1,0:T(8,128)(2,1)S(1)} %bitcast.17), kind=kOutput, calls=%fused_computation.2 | convolution fusion | flops 882769920 | bytes 6258688 | tf_op jit(solution)/shard_map/dot_general | solution.py:216
  33.5 0.1 slice-done
  33.6 0.1 slice-done.1
  33.7 1.9 %fusion.1 = bf16[896,192]{1,0:T(8,128)(2,1)S(1)} fusion(bf16[2560,896]{1,0:T(8,128)(2,1)S(1)} %bitcast.25, f32[896,192]{1,0:T(8,128)S(1)} %convolution_bitcast_fusion.1, bf16[2560,64]{1,0:T(8,128)(2,1)S(1)} %bitcast.20, bf16[2560,128]{1,0:T(8,128)(2,1)S(1)} %bitcast.18), kind=kOutput, calls=%fused_computation.4 | convolution fusion | flops 883802112 | bytes 6602752 | tf_op jit(solution)/shard_map/dot_general | solution.py:216
  35.6 0.7 slice.38.hidden
  36.3 0.7 slice.37.hidden
  37.0 15.4 %moment_pass.1 = (bf16[1,896,2560]{2,1,0:T(8,128)(2,1)}, bf16[896,2560]{1,0:T(8,128)(2,1)}, bf16[448,40]{1,0:T(8,128)(2,1)}) custom-call(bf16[896,128]{1,0:T(8,128)(2,1)} %slice.38.hidden, bf16[2560,128]{1,0:T(8,128)(2,1)} %bitcast.16, bf16[1,896,2560]{2,1,0:T(8,128)(2,1)} %momentum.1, s32[2,14,40,32]{3,2,1,0:T(8,128)} %copy.20.indices, ...), custom_call_target="tpu_custom_call" | custom-call | tf_op jit(solution)/shard_map/moment_pass/pallas_call | solution.py:289
  52.4 7.0 %exchange.1.values = bf16[1,448,40]{2,1,0:T(8,128)(2,1)} custom-call(bf16[448,40]{1,0:T(8,128)(2,1)} %get-tuple-element.6.values), custom_call_target="tpu_custom_call" | custom-call | tf_op jit(solution)/shard_map/exchange/pallas_call | solution.py:155
  59.5 10.3 %output_pass.1.parts = bf16[16,4,2560]{2,1,0:T(4,128)(2,1)} custom-call(bf16[896,64]{1,0:T(8,128)(2,1)} %slice.37.hidden, bf16[896,2560]{1,0:T(8,128)(2,1)} %down.1, bf16[896,2560]{1,0:T(8,128)(2,1)} %get-tuple-element.5.mine, bf16[1,448,40]{2,1,0:T(8,128)(2,1)} %exchange.1.values, s32[2,14,40,32]{3,2,1,0:T(8,128)} %copy.20.indices, ...), custom_call_target="tpu_custom_call" | custom-call | tf_op jit(solution)/shard_map/output_pass/pallas_call | solution.py:384
  69.8 10.8 %scatter_sum.1 = bf16[4,2560]{1,0:T(4,128)(2,1)} custom-call(bf16[16,4,2560]{2,1,0:T(4,128)(2,1)} %output_pass.1.parts), custom_call_target="tpu_custom_call" | custom-call | tf_op jit(solution)/shard_map/scatter_sum/pallas_call | solution.py:196
  80.5 1.3 %copy.25 = bf16[4,2560]{1,0:T(4,128)(2,1)} copy(bf16[4,2560]{1,0:T(4,128)(2,1)} %scatter_sum.1) | data formatting | bytes 40960
  (2 shorter events, 0.0 us)
Async XLA Ops:
  27.6 3.9 %copy-start = (bf16[2560,896]{1,0:T(8,128)(2,1)S(1)}, bf16[2560,896]{1,0:T(8,128)(2,1)}, u32[]{:S(2)}) copy-start(bf16[2560,896]{1,0:T(8,128)(2,1)} %param.18) | copy-start | bytes 13762564
  31.4 2.2 %slice-start = ((s8[4587520]{0:T(1024)(128)(4,1)}), s8[4194304]{0:T(1024)(128)(4,1)S(1)}, s32[]{:S(2)}) async-start(s8[4587520]{0:T(1024)(128)(4,1)} %bitcast.24), calls=%async_computation | async-start | bytes 8388608
  31.5 2.1 %slice-start.1 = ((s8[4587520]{0:T(1024)(128)(4,1)}), s8[393216]{0:T(1024)(128)(4,1)S(1)}, s32[]{:S(2)}) async-start(s8[4587520]{0:T(1024)(128)(4,1)} %bitcast.24), calls=%async_computation.1 | async-start | bytes 786432

commit v3 on v2

--- a/solution.py
+++ b/solution.py
@@ -58,78 +58,124 @@
     pl.semaphore_wait(barrier, len(others))
 
 
-def gather_kernel(size, block, out, send, recv, local):
+def hidden_kernel(
+    size, feature_block, grad_block, gate_weight, up_weight, grads, hidden, next_hidden,
+    held, features, turned, gate, upper, send, recv, local,
+):
     me = lax.axis_index("tensor")
     depth = size // 4
     z, x, core = me // 4, (me // 2) % 2, me % 2
+    blocks, kept = (feature_block, grad_block), (held, grads)
 
     def slot(zz, xx, cc):
         return (zz * 2 + xx) * 2 + cc
 
+    loads = [
+        pltpu.make_async_copy(source, target, local.at[n])
+        for n, (source, target) in enumerate(
+            [
+                (feature_block, held.at[me]),
+                (grad_block, grads.at[me]),
+                (gate_weight, gate),
+                (up_weight, upper),
+            ]
+        )
+    ]
+    for load in loads:
+        load.start()
     others = [flip(z, k) for k in range(1, depth)]
     side, twin = slot(z, 1 - x, core), slot(z, x, 1 - core)
     greet("tensor", [slot(zz, x, core) for zz in others] + [side, twin])
-    own = pltpu.make_async_copy(block, out.at[me], local)
-    own.start()
     copies = []
 
-    def push(source, which, target):
+    def push(kind, which, target, source=None):
         copy = pltpu.make_async_remote_copy(
-            src_ref=source,
-            dst_ref=out.at[which],
+            src_ref=kept[kind].at[which] if source is None else source,
+            dst_ref=kept[kind].at[which],
             send_sem=send.at[len(copies)],
-            recv_sem=recv.at[which],
+            recv_sem=recv.at[kind, which],
             device_id={"tensor": target},
             device_id_type=MESH,
         )
         copy.start()
         copies.append(copy)
 
-    def arrive(which):
+    def arrive(kind, which):
         pltpu.make_async_remote_copy(
-            src_ref=block,
-            dst_ref=out.at[which],
+            src_ref=blocks[kind],
+            dst_ref=kept[kind].at[which],
             send_sem=send.at[0],
-            recv_sem=recv.at[which],
+            recv_sem=recv.at[kind, which],
             device_id={"tensor": twin},
             device_id_type=MESH,
         ).wait_recv()
 
-    push(block, me, side)
-    for zz in others:
-        push(block, me, slot(zz, x, core))
-    push(block, me, twin)
-    for zz in others:
-        which = slot(zz, x, core)
-        arrive(which)
-        push(out.at[which], which, side)
-        push(out.at[which], which, twin)
+    for kind in range(2):
+        for target in [side] + [slot(zz, x, core) for zz in others] + [twin]:
+            push(kind, me, target, blocks[kind])
+    for kind in range(2):
+        for zz in others:
+            which = slot(zz, x, core)
+            arrive(kind, which)
+            push(kind, which, side)
+            push(kind, which, twin)
+    for kind in range(2):
+        for zz in [z] + others:
+            which = slot(zz, 1 - x, core)
+            arrive(kind, which)
+            push(kind, which, twin)
+    for load in loads:
+        load.wait()
     for zz in [z] + others:
-        which = slot(zz, 1 - x, core)
-        arrive(which)
-        push(out.at[which], which, twin)
+        arrive(0, slot(zz, x, 1 - core))
+        arrive(0, slot(zz, 1 - x, 1 - core))
+    share, count = grads.shape[1:]
+    nexts = next_hidden.shape[1]
+    split = share // 2
+    for n in range(size):
+        base = n * share
+        features[base : base + share, :count] = held[n, :share]
+        features[base : base + split, count:] = held[n, share:, :nexts]
+        features[base + split : base + share, count:] = held[n, share:, nexts:]
+    turned[...] = features[...].T
+    wide = dot(turned[...], gate[...])
+    mixed = (wide / (1.0 + jnp.exp(-wide)) * dot(turned[...], upper[...])).astype(jnp.bfloat16).T
+    hidden[...] = mixed[:, :count]
+    next_hidden[...] = mixed[:, count:]
     for zz in [z] + others:
-        arrive(slot(zz, x, 1 - core))
-        arrive(slot(zz, 1 - x, 1 - core))
-    own.wait()
+        arrive(1, slot(zz, x, 1 - core))
+        arrive(1, slot(zz, 1 - x, 1 - core))
     for copy in copies:
         copy.wait_send()
 
 
-def gather_blocks(block, size):
+def hidden_pass(feature_block, grad_block, gate_weight, up_weight, nexts, size):
+    share, count = grad_block.shape
+    breadth, width = gate_weight.shape
+    kind = jnp.bfloat16
+    hbm = pl.BlockSpec(memory_space=pl.ANY)
     return pl.pallas_call(
-        functools.partial(gather_kernel, size),
-        out_shape=jax.ShapeDtypeStruct((size,) + block.shape, block.dtype),
-        in_specs=[VMEM],
-        out_specs=VMEM,
+        functools.partial(hidden_kernel, size),
+        out_shape=(
+            jax.ShapeDtypeStruct((size, share, count), kind),
+            jax.ShapeDtypeStruct((width, count), kind),
+            jax.ShapeDtypeStruct((width, nexts), kind),
+        ),
+        in_specs=[VMEM, VMEM, hbm, hbm],
+        out_specs=(VMEM, VMEM, VMEM),
         scratch_shapes=[
-            pltpu.SemaphoreType.DMA((size,)),
-            pltpu.SemaphoreType.DMA((size,)),
-            pltpu.SemaphoreType.DMA,
+            pltpu.VMEM((size,) + feature_block.shape, kind),
+            pltpu.VMEM((breadth, count + nexts), kind),
+            pltpu.VMEM((count + nexts, breadth), kind),
+            pltpu.VMEM(gate_weight.shape, kind),
+            pltpu.VMEM(up_weight.shape, kind),
+            pltpu.SemaphoreType.DMA((2 * size,)),
+            pltpu.SemaphoreType.DMA((2, size)),
+            pltpu.SemaphoreType.DMA((4,)),
         ],
         compiler_params=pltpu.CompilerParams(collective_id=0, has_side_effects=True),
-        name="gather_blocks",
-    )(block)
+        name="hidden_pass",
+    )(feature_block, grad_block, gate_weight, up_weight)
 
 
 def exchange_kernel(replicas, values, out, send, recv):
@@ -223,12 +269,12 @@
 
 
 def strip_offsets(indices, which):
-    strip, columns, keep = indices.shape[1:]
-    first = lax.broadcasted_iota(jnp.int32, (columns, keep), 1) * (TILE * TILE // keep)
+    strip, keep, columns = indices.shape[1:]
+    first = lax.broadcasted_iota(jnp.int32, (keep, columns), 0) * (TILE * TILE // keep)
     listed = [
         (indices[which, n] - first).astype(jnp.float32).astype(jnp.bfloat16) for n in range(strip)
     ]
-    return jnp.concatenate(listed, axis=1)
+    return jnp.concatenate(listed, axis=0)
 
 
 def moment_kernel(
@@ -241,7 +287,7 @@
     spans = [slice(start, start + chunk) for start in range(0, breadth, chunk)]
     own_offsets = strip_offsets(indices, lax.axis_index("replica"))
     for span in spans:
-        offset[:, span] = contract(own_offsets, spread[:, span], 0)
+        offset[:, span] = dot(own_offsets, spread[:, span])
     for span in spans:
         moment[:, span] = BETA_DECAY * momentum[0, :, span].astype(jnp.float32) + contract(
             hidden[...], grads[span, :], 1
@@ -282,7 +328,7 @@
 def moment_pass(hidden, grads, momentum, indices, spread, mats, strip, chunk):
     rows, breadth = momentum.shape[1:]
     tall = strip * TILE
-    replicas, _, columns, keep = indices.shape
+    replicas, _, keep, columns = indices.shape
     half = strip * keep
     row, col_high, col_low, inverse_row, inverse_col = mats
     gather = spread.T
@@ -298,7 +344,7 @@
             pl.BlockSpec((tall, hidden.shape[1]), lambda i: (i, 0)),
             whole_block(grads),
             pl.BlockSpec((1, tall, breadth), lambda i: (0, i, 0)),
-            pl.BlockSpec((replicas, strip, columns, keep), lambda i: (0, i, 0, 0)),
+            pl.BlockSpec((replicas, strip, keep, columns), lambda i: (0, i, 0, 0)),
             whole_block(spread),
             whole_block(gather),
             whole_block(row),
@@ -332,7 +378,7 @@
     out, total, placed, wide, new,
 ):
     step = pl.program_id(0)
-    replicas, strip, _, keep = indices.shape
+    replicas, strip, keep, _ = indices.shape
     half = strip * keep
     tall, breadth = new.shape
     spans = [slice(start, start + chunk) for start in range(0, breadth, chunk)]
@@ -349,7 +395,7 @@
     for n, span in enumerate(spans):
         even = odd = 0.0
         for k in range(replicas - 1):
-            offset = contract(listed[k], spread[:, span], 0)
+            offset = dot(listed[k], spread[:, span])
             value = dot(values[k], spread[:, span])
             even = even + jnp.where(offset == place, value, 0.0)
             odd = odd + jnp.where(offset == place + TILE, value, 0.0)
@@ -377,7 +423,7 @@
 def output_pass(hidden, down, mine, values, indices, spread, mats, strip, chunk, size):
     rows, breadth = down.shape
     tall = strip * TILE
-    replicas, _, columns, keep = indices.shape
+    replicas, _, keep, columns = indices.shape
     half = strip * keep
     count = hidden.shape[1]
     inverse_row, inverse_col = mats[3:]
@@ -390,7 +436,7 @@
             pl.BlockSpec((tall, breadth), lambda i: (i, 0)),
             pl.BlockSpec((tall, breadth), lambda i: (i, 0)),
             pl.BlockSpec((replicas - 1, half, columns), lambda i: (0, i, 0)),
-            pl.BlockSpec((replicas, strip, columns, keep), lambda i: (0, i, 0, 0)),
+            pl.BlockSpec((replicas, strip, keep, columns), lambda i: (0, i, 0, 0)),
             whole_block(spread),
             whole_block(inverse_row),
             whole_block(inverse_col),
@@ -420,31 +466,21 @@
 
     turned = next_tokens.T
     block = jnp.concatenate(
-        [
-            cotangent.T,
-            tokens.T,
-            jnp.concatenate([turned[: share // 2], turned[share // 2 :]], axis=1),
-        ],
-        axis=0,
-    )
-    gathered = gather_blocks(block, size)
-    grads = gathered[:, :share].reshape(breadth, count)
-    features = gathered[:, share : 2 * share].reshape(breadth, count)
-    tail = gathered[:, 2 * share :]
-    next_features = jnp.concatenate([tail[:, :, :nexts], tail[:, :, nexts:]], axis=1)
-    features = jnp.concatenate([features, next_features.reshape(breadth, nexts)], axis=1)
-    gate = contract(gate_weight, features, 0)
-    upper = contract(up_weight, features, 0)
-    hidden = (jax.nn.silu(gate) * upper).astype(jnp.bfloat16)
-
+        [tokens.T, jnp.concatenate([turned[: share // 2], turned[share // 2 :]], axis=1)], axis=0
+    )
+    grads, hidden, next_hidden = hidden_pass(
+        block, cotangent.T, gate_weight, up_weight, nexts, size
+    )
+    grads = grads.reshape(breadth, count)
+    indices = jnp.swapaxes(indices, 2, 3)
     spread = jnp.asarray(np.kron(np.eye(tile_cols), np.ones((1, TILE))), jnp.bfloat16)
     mats = tables(strip, chunk)
     kept, mine, sent = moment_pass(
-        hidden[:, :count], grads, momentum, indices, spread, mats, strip, chunk
+        hidden, grads, momentum, indices, spread, mats, strip, chunk
     )
     values = exchange(sent, replicas)
     partial = output_pass(
-        hidden[:, count:], down_weight, mine, values, indices, spread, mats, strip, chunk, size
+        next_hidden, down_weight, mine, values, indices, spread, mats, strip, chunk, size
     )
     output = scatter_sum(partial)
     return (output, kept)

time: 82.6 us -> 70.8 us (0.86)
  local copies, waits for them, and re-layouts: 9.7 us -> 2.21 us
  matrix products: 3.83 us -> 0 us
    slice x4 -> x0, local copies, waits for them, and re-layouts: 5.17 us -> none  [the longest x1 2.38 us: on_device(): grads = gathered[:, :share].reshape(breadth, count)]
    dot_general x2 -> x0, matrix products: 3.83 us -> none  [contract(): lax.dot_general(a, b, (((dim,), (dim,)), ((), ())), preferred_element_typ...]
    unnamed x9 -> x2, local copies, waits for them, and re-layouts: 4.52 us -> 2.21 us
    pallas_call x1, Pallas kernels: 22.5 us -> 23.8 us  [hidden_pass(): pl.pallas_call(functools.partial(hidden_kernel, size), out_shape=(jax.Sha...]
    pallas_call x1, Pallas kernels: 15.4 us -> 14.6 us  [moment_pass(): pl.pallas_call(functools.partial(moment_kernel, chunk), grid=(rows // tal...]
    concatenate x2 -> x1, other arithmetic: 1.66 us -> 1.49 us  [on_device(): jnp.concatenate([tokens.T, jnp.concatenate([turned[:share // 2], turned[s...]
where the time goes in v3:
time: 70.8 us; the launch traced here: 70 us
  Pallas kernels  65.7 us (93%)
  local copies, waits for them, and re-layouts  2.21 us (3%)
  other arithmetic  1.49 us (2%)
    pallas_call x1, Pallas kernels, hidden_pass(): pl.pallas_call(functools.partial(hidden_kernel, size), out_shape=(jax.Sha...  23.8 us
    pallas_call x1, Pallas kernels, moment_pass(): pl.pallas_call(functools.partial(moment_kernel, chunk), grid=(rows // tal...  14.6 us
    pallas_call x1, Pallas kernels, scatter_sum(): pl.pallas_call(functools.partial(scatter_kernel, size), out_shape=jax.Sha...  10.8 us
    pallas_call x1, Pallas kernels, output_pass(): pl.pallas_call(functools.partial(output_kernel, chunk), grid=(rows // tal...  10.1 us
    pallas_call x1, Pallas kernels, exchange(): pl.pallas_call(functools.partial(exchange_kernel, replicas), out_shape=ja...  6.39 us
    unnamed x2, local copies, waits for them, and re-layouts  2.21 us
    concatenate x1, other arithmetic, on_device(): jnp.concatenate([tokens.T, jnp.concatenate([turned[:share // 2], turned[s...  1.49 us

profile of v3, /device:TPU:0, one launch (start us, length us, event | category | flops | bytes accessed | tf_op | source)
XLA Modules:
  0.0 70.0 jit_solution(17598812165534513679)
XLA Ops:
  0.6 0.9 %copy.17 = bf16[64,160]{0,1:T(8,128)(2,1)S(1)} copy(bf16[64,160]{1,0:T(8,128)(2,1)} %param.16) | data formatting | bytes 40960 | tf_op args[1]
  1.5 1.5 %maximum_maximum_fusion.feature_block = bf16[240,128]{1,0:T(8,128)(2,1)} fusion(bf16[80,64]{1,0:T(8,128)(2,1)S(1)} %get-tuple-element.15, bf16[80,64]{1,0:T(8,128)(2,1)S(1)} %get-tuple-element.14, bf16[160,128]{1,0:T(8,128)(2,1)} %bitcast.9), kind=kLoop, calls=%fused_computation | loop fusion | flops 184320 | bytes 122880 | tf_op jit(solution)/shard_map/concatenate | solution.py:468
  3.0 23.8 %hidden_pass.1 = (bf16[16,160,128]{2,1,0:T(8,128)(2,1)}, bf16[896,128]{1,0:T(8,128)(2,1)}, bf16[896,64]{1,0:T(8,128)(2,1)}) custom-call(bf16[240,128]{1,0:T(8,128)(2,1)} %maximum_maximum_fusion.feature_block, bf16[160,128]{1,0:T(8,128)(2,1)} %bitcast.10, bf16[2560,896]{1,0:T(8,128)(2,1)} %gate_weight.1, bf16[2560,896]{1,0:T(8,128)(2,1)} %up_weight.1), custom_call_target="tpu_custom_call" | custom-call | tf_op jit(solution)/shard_map/hidden_pass/pallas_call | solution.py:157
  26.8 14.6 %moment_pass.1 = (bf16[1,896,2560]{2,1,0:T(8,128)(2,1)}, bf16[896,2560]{1,0:T(8,128)(2,1)}, bf16[448,40]{1,0:T(8,128)(2,1)}) custom-call(bf16[896,128]{1,0:T(8,128)(2,1)} %get-tuple-element.9.hidden, bf16[2560,128]{1,0:T(8,128)(2,1)} %bitcast.7, bf16[1,896,2560]{2,1,0:T(8,128)(2,1)} %momentum.1, s32[2,14,32,40]{3,2,1,0:T(8,128)} %bitcast.5, ...), custom_call_target="tpu_custom_call" | custom-call | tf_op jit(solution)/shard_map/moment_pass/pallas_call | solution.py:335
  41.4 6.4 %exchange.1.values = bf16[1,448,40]{2,1,0:T(8,128)(2,1)} custom-call(bf16[448,40]{1,0:T(8,128)(2,1)} %get-tuple-element.12.values), custom_call_target="tpu_custom_call" | custom-call | tf_op jit(solution)/shard_map/exchange/pallas_call | solution.py:201
  47.8 10.1 %output_pass.1.parts = bf16[16,4,2560]{2,1,0:T(4,128)(2,1)} custom-call(bf16[896,64]{1,0:T(8,128)(2,1)} %get-tuple-element.8.hidden, bf16[896,2560]{1,0:T(8,128)(2,1)} %down.1, bf16[896,2560]{1,0:T(8,128)(2,1)} %get-tuple-element.11.mine, bf16[1,448,40]{2,1,0:T(8,128)(2,1)} %exchange.1.values, s32[2,14,32,40]{3,2,1,0:T(8,128)} %bitcast.6, ...), custom_call_target="tpu_custom_call" | custom-call | tf_op jit(solution)/shard_map/output_pass/pallas_call | solution.py:430
  57.9 10.8 %scatter_sum.1 = bf16[4,2560]{1,0:T(4,128)(2,1)} custom-call(bf16[16,4,2560]{2,1,0:T(4,128)(2,1)} %output_pass.1.parts), custom_call_target="tpu_custom_call" | custom-call | tf_op jit(solution)/shard_map/scatter_sum/pallas_call | solution.py:242
  68.7 1.3 %copy.19 = bf16[4,2560]{1,0:T(4,128)(2,1)} copy(bf16[4,2560]{1,0:T(4,128)(2,1)} %scatter_sum.1) | data formatting | bytes 40960
  (1 shorter events, 0.0 us)

commit v4 on v3

--- a/solution.py
+++ b/solution.py
@@ -178,82 +178,6 @@
     )(feature_block, grad_block, gate_weight, up_weight)
 
 
-def exchange_kernel(replicas, values, out, send, recv):
-    me = lax.axis_index("replica")
-    greet("replica", [(me + k) % replicas for k in range(1, replicas)])
-    copies = []
-    for k in range(1, replicas):
-        copy = pltpu.make_async_remote_copy(
-            src_ref=values,
-            dst_ref=out.at[k - 1],
-            send_sem=send.at[k - 1],
-            recv_sem=recv.at[k - 1],
-            device_id={"replica": (me - k + replicas) % replicas},
-            device_id_type=MESH,
-        )
-        copy.start()
-        copies.append(copy)
-    for copy in copies:
-        copy.wait()
-
-
-def exchange(values, replicas):
-    return pl.pallas_call(
-        functools.partial(exchange_kernel, replicas),
-        out_shape=jax.ShapeDtypeStruct((replicas - 1,) + values.shape, values.dtype),
-        in_specs=[VMEM],
-        out_specs=VMEM,
-        scratch_shapes=[
-            pltpu.SemaphoreType.DMA((replicas - 1,)),
-            pltpu.SemaphoreType.DMA((replicas - 1,)),
-        ],
-        compiler_params=pltpu.CompilerParams(collective_id=1, has_side_effects=True),
-        name="exchange",
-    )(values)
-
-
-def scatter_kernel(size, parts, out, held, send, recv):
-    me = lax.axis_index("tensor")
-    greet("tensor", [(me + k) % size for k in range(1, size)])
-    copies = []
-    for k in range(1, size):
-        target = (me + k) % size
-        copy = pltpu.make_async_remote_copy(
-            src_ref=parts.at[target],
-            dst_ref=held.at[k - 1],
-            send_sem=send.at[k - 1],
-            recv_sem=recv.at[k - 1],
-            device_id={"tensor": target},
-            device_id_type=MESH,
-        )
-        copy.start()
-        copies.append(copy)
-    total = parts[me].astype(jnp.float32)
-    for k in range(1, size):
-        copies[k - 1].wait_recv()
-        total = total + held[k - 1].astype(jnp.float32)
-    out[...] = total.astype(out.dtype)
-    for copy in copies:
-        copy.wait_send()
-
-
-def scatter_sum(parts):
-    size = parts.shape[0]
-    return pl.pallas_call(
-        functools.partial(scatter_kernel, size),
-        out_shape=jax.ShapeDtypeStruct(parts.shape[1:], parts.dtype),
-        in_specs=[VMEM],
-        out_specs=VMEM,
-        scratch_shapes=[
-            pltpu.VMEM((size - 1,) + parts.shape[1:], parts.dtype),
-            pltpu.SemaphoreType.DMA((size - 1,)),
-            pltpu.SemaphoreType.DMA((size - 1,)),
-        ],
-        compiler_params=pltpu.CompilerParams(collective_id=2, has_side_effects=True),
-        name="scatter_sum",
-    )(parts)
-
-
 def dot(a, b):
     return jnp.dot(a, b, preferred_element_type=jnp.float32)
 
@@ -279,10 +203,19 @@
 
 def moment_kernel(
     chunk, hidden, grads, momentum, indices, spread, gather, row, col_high, col_low,
-    inverse_row, inverse_col, kept, mine, sent,
-    moment, mixed, offset, picked, stacked, pair,
+    inverse_row, inverse_col, kept, mine, values_out,
+    moment, mixed, offset, picked, stacked, pair, sent, received, send, recv,
 ):
     tall, breadth = moment.shape
+    step = pl.program_id(0)
+    replicas = indices.shape[0]
+    steps = sent.shape[0]
+    replica = lax.axis_index("replica")
+
+    @pl.when(step == 0)
+    def _():
+        greet("replica", [(replica + k) % replicas for k in range(1, replicas)])
+
     half = tall // 2
     spans = [slice(start, start + chunk) for start in range(0, breadth, chunk)]
     own_offsets = strip_offsets(indices, lax.axis_index("replica"))
@@ -309,7 +242,7 @@
         ).astype(jnp.bfloat16)
         picked[:, span] = values
         stacked[k * half : (k + 1) * half] = values
-    sent[...] = dot(picked[...], gather[...]).astype(jnp.bfloat16)
+    sent[step] = dot(picked[...], gather[...]).astype(jnp.bfloat16)
     for k, span in enumerate(spans):
         wide = dot(stacked[k * half : (k + 1) * half], inverse_col[...])
         odd = offset[:, span] >= TILE
@@ -319,6 +252,26 @@
         own = dot(inverse_row[...], pair[:, span])
         kept[0, :, span] = (moment[:, span] - own).astype(jnp.bfloat16)
         mine[:, span] = own.astype(jnp.bfloat16)
+
+    def transfer(which, k):
+        return pltpu.make_async_remote_copy(
+            src_ref=sent.at[which],
+            dst_ref=received.at[k - 1, which],
+            send_sem=send.at[k - 1, which],
+            recv_sem=recv.at[k - 1, which],
+            device_id={"replica": (replica - k + replicas) % replicas},
+            device_id_type=MESH,
+        )
+
+    for k in range(1, replicas):
+        transfer(step, k).start()
+
+    @pl.when(step == steps - 1)
+    def _():
+        for k in range(1, replicas):
+            for which in range(steps):
+                transfer(which, k).wait()
+                values_out[k - 1, which] = received[k - 1, which]
 
 
 def whole_block(array):
@@ -338,7 +291,7 @@
         out_shape=(
             jax.ShapeDtypeStruct((1, rows, breadth), jnp.bfloat16),
             jax.ShapeDtypeStruct((rows, breadth), jnp.bfloat16),
-            jax.ShapeDtypeStruct((rows // 2, columns), jnp.bfloat16),
+            jax.ShapeDtypeStruct((replicas - 1, rows // tall, half, columns), jnp.bfloat16),
         ),
         in_specs=[
             pl.BlockSpec((tall, hidden.shape[1]), lambda i: (i, 0)),
@@ -356,7 +309,9 @@
         out_specs=(
             pl.BlockSpec((1, tall, breadth), lambda i: (0, i, 0)),
             pl.BlockSpec((tall, breadth), lambda i: (i, 0)),
-            pl.BlockSpec((half, columns), lambda i: (i, 0)),
+            pl.BlockSpec(
+                (replicas - 1, rows // tall, half, columns), lambda i: (0, 0, 0, 0)
+            ),
         ),
         scratch_shapes=[
             pltpu.VMEM((tall, breadth), jnp.float32),
@@ -365,7 +320,12 @@
             pltpu.VMEM((half, breadth), jnp.bfloat16),
             pltpu.VMEM((half * (breadth // chunk), chunk), jnp.bfloat16),
             pltpu.VMEM((tall, breadth), jnp.bfloat16),
+            pltpu.VMEM((rows // tall, half, columns), jnp.bfloat16),
+            pltpu.VMEM((replicas - 1, rows // tall, half, columns), jnp.bfloat16),
+            pltpu.SemaphoreType.DMA((replicas - 1, rows // tall)),
+            pltpu.SemaphoreType.DMA((replicas - 1, rows // tall)),
         ],
+        compiler_params=pltpu.CompilerParams(collective_id=1, has_side_effects=True),
         name="moment_pass",
     )(
         hidden, grads, momentum, indices, spread, gather, row, col_high, col_low, inverse_row,
@@ -374,24 +334,30 @@
 
 
 def output_kernel(
-    chunk, hidden, down, mine, values, indices, spread, inverse_row, inverse_col,
-    out, total, placed, wide, new,
+    chunk, size, hidden, down, mine, values, indices, spread, inverse_row, inverse_col,
+    out, placed, wide, new, stage, held, send, recv,
 ):
     step = pl.program_id(0)
-    replicas, strip, keep, _ = indices.shape
-    half = strip * keep
-    tall, breadth = new.shape
+    steps = stage.shape[0]
+    replicas = indices.shape[0]
+    rows, breadth = new.shape
+    tall = inverse_row.shape[0]
+    half = tall // 2
+    strips = rows // tall
     spans = [slice(start, start + chunk) for start in range(0, breadth, chunk)]
     replica = lax.axis_index("replica")
+    me = lax.axis_index("tensor")
+    barrier = pltpu.get_barrier_semaphore()
 
     @pl.when(step == 0)
     def _():
-        total[...] = jnp.zeros_like(total)
-
-    place = lanes((half, chunk)).astype(jnp.float32)
-    listed = [
-        strip_offsets(indices, (replica + k) % replicas) for k in range(1, replicas)
-    ]
+        for k in range(1, size):
+            pl.semaphore_signal(
+                barrier, inc=1, device_id={"tensor": (me + k) % size}, device_id_type=MESH
+            )
+
+    place = lanes((rows // 2, chunk)).astype(jnp.float32)
+    listed = [strip_offsets(indices, (replica + k) % replicas) for k in range(1, replicas)]
     for n, span in enumerate(spans):
         even = odd = 0.0
         for k in range(replicas - 1):
@@ -399,55 +365,87 @@
             value = dot(values[k], spread[:, span])
             even = even + jnp.where(offset == place, value, 0.0)
             odd = odd + jnp.where(offset == place + TILE, value, 0.0)
-        placed[n * tall : n * tall + half] = even.astype(jnp.bfloat16)
-        placed[n * tall + half : (n + 1) * tall] = odd.astype(jnp.bfloat16)
+        even, odd = even.astype(jnp.bfloat16), odd.astype(jnp.bfloat16)
+        for m in range(strips):
+            base = n * rows + m * tall
+            placed[base : base + half] = even[m * half : (m + 1) * half]
+            placed[base + half : base + tall] = odd[m * half : (m + 1) * half]
     for n, span in enumerate(spans):
-        wide[:, span] = dot(placed[n * tall : (n + 1) * tall], inverse_col[...]).astype(
+        wide[:, span] = dot(placed[n * rows : (n + 1) * rows], inverse_col[...]).astype(
             jnp.bfloat16
         )
-    for span in spans:
-        update = mine[:, span].astype(jnp.float32) + dot(inverse_row[...], wide[:, span])
-        new[:, span] = (
-            down[:, span].astype(jnp.float32) - (STEP_RATE / replicas) * update
+    for m in range(strips):
+        band = slice(m * tall, (m + 1) * tall)
+        update = mine[band].astype(jnp.float32) + dot(inverse_row[...], wide[band])
+        new[band] = (
+            down[band].astype(jnp.float32) - (STEP_RATE / replicas) * update
         ).astype(jnp.bfloat16)
-    for span in spans:
-        total[:, span] += contract(hidden[...], new[:, span], 0)
-
-    @pl.when(step == pl.num_programs(0) - 1)
+    part = contract(hidden[...], new[...], 0).astype(jnp.bfloat16)
+    short = out.shape[0]
+    for n in range(size):
+        stage[step, n] = part[n * short : (n + 1) * short]
+
+    @pl.when(step == 0)
     def _():
-        size, rows, _ = out.shape
-        for n in range(size):
-            out[n] = total[n * rows : (n + 1) * rows].astype(out.dtype)
-
-
-def output_pass(hidden, down, mine, values, indices, spread, mats, strip, chunk, size):
+        pl.semaphore_wait(barrier, size - 1)
+
+    def transfer(which, k):
+        target = (me + k) % size
+        return pltpu.make_async_remote_copy(
+            src_ref=stage.at[which, target],
+            dst_ref=held.at[which, k - 1],
+            send_sem=send.at[which, k - 1],
+            recv_sem=recv.at[which, k - 1],
+            device_id={"tensor": target},
+            device_id_type=MESH,
+        )
+
+    for k in range(1, size):
+        transfer(step, k).start()
+
+    @pl.when(step == steps - 1)
+    def _():
+        for which in range(steps):
+            total = stage[which, me].astype(jnp.float32)
+            for k in range(1, size):
+                transfer(which, k).wait()
+                total = total + held[which, k - 1].astype(jnp.float32)
+            out[:, which * breadth : (which + 1) * breadth] = total.astype(out.dtype)
+
+
+def output_pass(hidden, down, mine, values, indices, spread, mats, chunk, size):
     rows, breadth = down.shape
-    tall = strip * TILE
-    replicas, _, keep, columns = indices.shape
-    half = strip * keep
-    count = hidden.shape[1]
+    columns = spread.shape[0]
+    part = 2 * chunk if breadth % (2 * chunk) == 0 else chunk
+    steps = breadth // part
+    short = hidden.shape[1] // size
     inverse_row, inverse_col = mats[3:]
+    kind = jnp.bfloat16
     return pl.pallas_call(
-        functools.partial(output_kernel, chunk),
-        grid=(rows // tall,),
-        out_shape=jax.ShapeDtypeStruct((size, count // size, breadth), jnp.bfloat16),
+        functools.partial(output_kernel, chunk, size),
+        grid=(steps,),
+        out_shape=jax.ShapeDtypeStruct((short, breadth), kind),
         in_specs=[
-            pl.BlockSpec((tall, count), lambda i: (i, 0)),
-            pl.BlockSpec((tall, breadth), lambda i: (i, 0)),
-            pl.BlockSpec((tall, breadth), lambda i: (i, 0)),
-            pl.BlockSpec((replicas - 1, half, columns), lambda i: (0, i, 0)),
-            pl.BlockSpec((replicas, strip, keep, columns), lambda i: (0, i, 0, 0)),
-            whole_block(spread),
+            whole_block(hidden),
+            pl.BlockSpec((rows, part), lambda i: (0, i)),
+            pl.BlockSpec((rows, part), lambda i: (0, i)),
+            whole_block(values),
+            whole_block(indices),
+            pl.BlockSpec((columns, part), lambda i: (0, i)),
             whole_block(inverse_row),
             whole_block(inverse_col),
         ],
-        out_specs=pl.BlockSpec((size, count // size, breadth), lambda i: (0, 0, 0)),
+        out_specs=pl.BlockSpec((short, breadth), lambda i: (0, 0)),
         scratch_shapes=[
-            pltpu.VMEM((count, breadth), jnp.float32),
-            pltpu.VMEM((tall * (breadth // chunk), chunk), jnp.bfloat16),
-            pltpu.VMEM((tall, breadth), jnp.bfloat16),
-            pltpu.VMEM((tall, breadth), jnp.bfloat16),
+            pltpu.VMEM((rows * (part // chunk), chunk), kind),
+            pltpu.VMEM((rows, part), kind),
+            pltpu.VMEM((rows, part), kind),
+            pltpu.VMEM((steps, size, short, part), kind),
+            pltpu.VMEM((steps, size - 1, short, part), kind),
+            pltpu.SemaphoreType.DMA((steps, size - 1)),
+            pltpu.SemaphoreType.DMA((steps, size - 1)),
         ],
+        compiler_params=pltpu.CompilerParams(collective_id=2, has_side_effects=True),
         name="output_pass",
     )(hidden, down, mine, values, indices, spread, inverse_row, inverse_col)
 
@@ -475,14 +473,13 @@
     indices = jnp.swapaxes(indices, 2, 3)
     spread = jnp.asarray(np.kron(np.eye(tile_cols), np.ones((1, TILE))), jnp.bfloat16)
     mats = tables(strip, chunk)
-    kept, mine, sent = moment_pass(
+    kept, mine, values = moment_pass(
         hidden, grads, momentum, indices, spread, mats, strip, chunk
     )
-    values = exchange(sent, replicas)
-    partial = output_pass(
-        next_hidden, down_weight, mine, values, indices, spread, mats, strip, chunk, size
-    )
-    output = scatter_sum(partial)
+    values = values.reshape(replicas - 1, tile_rows * keep, tile_cols)
+    output = output_pass(
+        next_hidden, down_weight, mine, values, indices, spread, mats, chunk, size
+    )
     return (output, kept)
 
 

time: 70.8 us -> 67.9 us (0.959)
  Pallas kernels: 65.7 us -> 58.3 us
  local copies, waits for them, and re-layouts: 2.21 us -> 6.95 us
    pallas_call x3 -> x1, Pallas kernels: 27.3 us -> 15.9 us  [output_pass(): pl.pallas_call(functools.partial(output_kernel, chunk, size), grid=(steps...]
    unnamed x2 -> x3, local copies, waits for them, and re-layouts: 2.21 us -> 6.94 us
    pallas_call x1, Pallas kernels: 14.6 us -> 18.6 us  [moment_pass(): pl.pallas_call(functools.partial(moment_kernel, chunk), grid=(rows // tal...]
where the time goes in v4:
time: 67.9 us; the launch traced here: 67.4 us
  Pallas kernels  58.3 us (86%)
  local copies, waits for them, and re-layouts  6.95 us (10%)
  other arithmetic  1.49 us (2%)
    pallas_call x1, Pallas kernels, hidden_pass(): pl.pallas_call(functools.partial(hidden_kernel, size), out_shape=(jax.Sha...  23.8 us
    pallas_call x1, Pallas kernels, moment_pass(): pl.pallas_call(functools.partial(moment_kernel, chunk), grid=(rows // tal...  18.6 us
    pallas_call x1, Pallas kernels, output_pass(): pl.pallas_call(functools.partial(output_kernel, chunk, size), grid=(steps...  15.9 us
    unnamed x3, local copies, waits for them, and re-layouts  6.94 us
    concatenate x1, other arithmetic, on_device(): jnp.concatenate([tokens.T, jnp.concatenate([turned[:share // 2], turned[s...  1.49 us

profile of v4, /device:TPU:0, one launch (start us, length us, event | category | flops | bytes accessed | tf_op | source)
XLA Modules:
  0.0 67.4 jit_solution(16239114018021980147)
XLA Ops:
  0.6 0.9 %copy.17 = bf16[64,160]{0,1:T(8,128)(2,1)S(1)} copy(bf16[64,160]{1,0:T(8,128)(2,1)} %param.16) | data formatting | bytes 40960 | tf_op args[1]
  1.5 1.5 %maximum_maximum_fusion.feature_block = bf16[240,128]{1,0:T(8,128)(2,1)} fusion(bf16[80,64]{1,0:T(8,128)(2,1)S(1)} %get-tuple-element.15, bf16[80,64]{1,0:T(8,128)(2,1)S(1)} %get-tuple-element.14, bf16[160,128]{1,0:T(8,128)(2,1)} %bitcast.11), kind=kLoop, calls=%fused_computation | loop fusion | flops 184320 | bytes 122880 | tf_op jit(solution)/shard_map/concatenate | solution.py:466
  3.0 23.8 %hidden_pass.1 = (bf16[16,160,128]{2,1,0:T(8,128)(2,1)}, bf16[896,128]{1,0:T(8,128)(2,1)}, bf16[896,64]{1,0:T(8,128)(2,1)}) custom-call(bf16[240,128]{1,0:T(8,128)(2,1)} %maximum_maximum_fusion.feature_block, bf16[160,128]{1,0:T(8,128)(2,1)} %bitcast.12, bf16[2560,896]{1,0:T(8,128)(2,1)} %gate_weight.1, bf16[2560,896]{1,0:T(8,128)(2,1)} %up_weight.1), custom_call_target="tpu_custom_call" | custom-call | tf_op jit(solution)/shard_map/hidden_pass/pallas_call | solution.py:157
  26.8 18.6 %moment_pass.1 = (bf16[1,896,2560]{2,1,0:T(8,128)(2,1)}, bf16[896,2560]{1,0:T(8,128)(2,1)}, bf16[1,7,64,40]{3,2,1,0:T(8,128)(2,1)}) custom-call(bf16[896,128]{1,0:T(8,128)(2,1)} %get-tuple-element.9.hidden, bf16[2560,128]{1,0:T(8,128)(2,1)} %bitcast.8, bf16[1,896,2560]{2,1,0:T(8,128)(2,1)} %momentum.1, s32[2,14,32,40]{3,2,1,0:T(8,128)} %bitcast.6, ...), custom_call_target="tpu_custom_call" | custom-call | tf_op jit(solution)/shard_map/moment_pass/pallas_call | solution.py:288
  45.4 15.9 %output_pass.1 = bf16[4,2560]{1,0:T(4,128)(2,1)} custom-call(bf16[896,64]{1,0:T(8,128)(2,1)} %get-tuple-element.8.hidden, bf16[896,2560]{1,0:T(8,128)(2,1)} %down.1, bf16[896,2560]{1,0:T(8,128)(2,1)} %get-tuple-element.11.mine, bf16[1,448,40]{2,1,0:T(8,128)(2,1)} %bitcast.10, s32[2,14,32,40]{3,2,1,0:T(8,128)} %bitcast.7, ...), custom_call_target="tpu_custom_call" | custom-call | tf_op jit(solution)/shard_map/output_pass/pallas_call | solution.py:424
  61.3 1.3 %copy.20 = bf16[4,2560]{1,0:T(4,128)(2,1)} copy(bf16[4,2560]{1,0:T(4,128)(2,1)} %output_pass.1) | data formatting | bytes 40960
  62.7 4.7 %copy.21 = bf16[1,896,2560]{2,1,0:T(8,128)(2,1)} copy(bf16[1,896,2560]{2,1,0:T(8,128)(2,1)} %get-tuple-element.19) | data formatting | bytes 9175040
  (1 shorter events, 0.0 us)

commit v5 on v4

--- a/solution.py
+++ b/solution.py
@@ -203,19 +203,10 @@
 
 def moment_kernel(
     chunk, hidden, grads, momentum, indices, spread, gather, row, col_high, col_low,
-    inverse_row, inverse_col, kept, mine, values_out,
-    moment, mixed, offset, picked, stacked, pair, sent, received, send, recv,
+    inverse_row, inverse_col, kept, mine, sent,
+    moment, mixed, offset, picked, stacked, pair,
 ):
     tall, breadth = moment.shape
-    step = pl.program_id(0)
-    replicas = indices.shape[0]
-    steps = sent.shape[0]
-    replica = lax.axis_index("replica")
-
-    @pl.when(step == 0)
-    def _():
-        greet("replica", [(replica + k) % replicas for k in range(1, replicas)])
-
     half = tall // 2
     spans = [slice(start, start + chunk) for start in range(0, breadth, chunk)]
     own_offsets = strip_offsets(indices, lax.axis_index("replica"))
@@ -242,7 +233,7 @@
         ).astype(jnp.bfloat16)
         picked[:, span] = values
         stacked[k * half : (k + 1) * half] = values
-    sent[step] = dot(picked[...], gather[...]).astype(jnp.bfloat16)
+    sent[...] = dot(picked[...], gather[...]).astype(jnp.bfloat16)
     for k, span in enumerate(spans):
         wide = dot(stacked[k * half : (k + 1) * half], inverse_col[...])
         odd = offset[:, span] >= TILE
@@ -252,26 +243,6 @@
         own = dot(inverse_row[...], pair[:, span])
         kept[0, :, span] = (moment[:, span] - own).astype(jnp.bfloat16)
         mine[:, span] = own.astype(jnp.bfloat16)
-
-    def transfer(which, k):
-        return pltpu.make_async_remote_copy(
-            src_ref=sent.at[which],
-            dst_ref=received.at[k - 1, which],
-            send_sem=send.at[k - 1, which],
-            recv_sem=recv.at[k - 1, which],
-            device_id={"replica": (replica - k + replicas) % replicas},
-            device_id_type=MESH,
-        )
-
-    for k in range(1, replicas):
-        transfer(step, k).start()
-
-    @pl.when(step == steps - 1)
-    def _():
-        for k in range(1, replicas):
-            for which in range(steps):
-                transfer(which, k).wait()
-                values_out[k - 1, which] = received[k - 1, which]
 
 
 def whole_block(array):
@@ -291,7 +262,7 @@
         out_shape=(
             jax.ShapeDtypeStruct((1, rows, breadth), jnp.bfloat16),
             jax.ShapeDtypeStruct((rows, breadth), jnp.bfloat16),
-            jax.ShapeDtypeStruct((replicas - 1, rows // tall, half, columns), jnp.bfloat16),
+            jax.ShapeDtypeStruct((rows // 2, columns), jnp.bfloat16),
         ),
         in_specs=[
             pl.BlockSpec((tall, hidden.shape[1]), lambda i: (i, 0)),
@@ -309,9 +280,7 @@
         out_specs=(
             pl.BlockSpec((1, tall, breadth), lambda i: (0, i, 0)),
             pl.BlockSpec((tall, breadth), lambda i: (i, 0)),
-            pl.BlockSpec(
-                (replicas - 1, rows // tall, half, columns), lambda i: (0, 0, 0, 0)
-            ),
+            pl.BlockSpec((half, columns), lambda i: (i, 0)),
         ),
         scratch_shapes=[
             pltpu.VMEM((tall, breadth), jnp.float32),
@@ -320,12 +289,7 @@
             pltpu.VMEM((half, breadth), jnp.bfloat16),
             pltpu.VMEM((half * (breadth // chunk), chunk), jnp.bfloat16),
             pltpu.VMEM((tall, breadth), jnp.bfloat16),
-            pltpu.VMEM((rows // tall, half, columns), jnp.bfloat16),
-            pltpu.VMEM((replicas - 1, rows // tall, half, columns), jnp.bfloat16),
-            pltpu.SemaphoreType.DMA((replicas - 1, rows // tall)),
-            pltpu.SemaphoreType.DMA((replicas - 1, rows // tall)),
         ],
-        compiler_params=pltpu.CompilerParams(collective_id=1, has_side_effects=True),
         name="moment_pass",
     )(
         hidden, grads, momentum, indices, spread, gather, row, col_high, col_low, inverse_row,
@@ -335,7 +299,7 @@
 
 def output_kernel(
     chunk, size, hidden, down, mine, values, indices, spread, inverse_row, inverse_col,
-    out, placed, wide, new, stage, held, send, recv,
+    out, placed, wide, new, stage, held, send, recv, offset, received, pass_send, pass_recv,
 ):
     step = pl.program_id(0)
     steps = stage.shape[0]
@@ -349,22 +313,48 @@
     me = lax.axis_index("tensor")
     barrier = pltpu.get_barrier_semaphore()
 
+    def share(k):
+        return pltpu.make_async_remote_copy(
+            src_ref=values,
+            dst_ref=received.at[k - 1],
+            send_sem=pass_send.at[k - 1],
+            recv_sem=pass_recv.at[k - 1],
+            device_id={"replica": (replica - k + replicas) % replicas},
+            device_id_type=MESH,
+        )
+
     @pl.when(step == 0)
     def _():
         for k in range(1, size):
             pl.semaphore_signal(
                 barrier, inc=1, device_id={"tensor": (me + k) % size}, device_id_type=MESH
             )
+        for k in range(1, replicas):
+            pl.semaphore_signal(
+                barrier, inc=1, device_id={"replica": (replica + k) % replicas},
+                device_id_type=MESH,
+            )
+        pl.semaphore_wait(barrier, size + replicas - 2)
+        for k in range(1, replicas):
+            share(k).start()
 
     place = lanes((rows // 2, chunk)).astype(jnp.float32)
     listed = [strip_offsets(indices, (replica + k) % replicas) for k in range(1, replicas)]
+    for k in range(replicas - 1):
+        offset[k] = dot(listed[k], spread[...])
+
+    @pl.when(step == 0)
+    def _():
+        for k in range(1, replicas):
+            share(k).wait()
+
     for n, span in enumerate(spans):
         even = odd = 0.0
         for k in range(replicas - 1):
-            offset = dot(listed[k], spread[:, span])
-            value = dot(values[k], spread[:, span])
-            even = even + jnp.where(offset == place, value, 0.0)
-            odd = odd + jnp.where(offset == place + TILE, value, 0.0)
+            where = offset[k, :, span]
+            value = dot(received[k], spread[:, span])
+            even = even + jnp.where(where == place, value, 0.0)
+            odd = odd + jnp.where(where == place + TILE, value, 0.0)
         even, odd = even.astype(jnp.bfloat16), odd.astype(jnp.bfloat16)
         for m in range(strips):
             base = n * rows + m * tall
@@ -384,10 +374,6 @@
     short = out.shape[0]
     for n in range(size):
         stage[step, n] = part[n * short : (n + 1) * short]
-
-    @pl.when(step == 0)
-    def _():
-        pl.semaphore_wait(barrier, size - 1)
 
     def transfer(which, k):
         target = (me + k) % size
@@ -444,6 +430,10 @@
             pltpu.VMEM((steps, size - 1, short, part), kind),
             pltpu.SemaphoreType.DMA((steps, size - 1)),
             pltpu.SemaphoreType.DMA((steps, size - 1)),
+            pltpu.VMEM((indices.shape[0] - 1, rows // 2, part), jnp.float32),
+            pltpu.VMEM((indices.shape[0] - 1,) + values.shape, kind),
+            pltpu.SemaphoreType.DMA((indices.shape[0] - 1,)),
+            pltpu.SemaphoreType.DMA((indices.shape[0] - 1,)),
         ],
         compiler_params=pltpu.CompilerParams(collective_id=2, has_side_effects=True),
         name="output_pass",
@@ -476,7 +466,6 @@
     kept, mine, values = moment_pass(
         hidden, grads, momentum, indices, spread, mats, strip, chunk
     )
-    values = values.reshape(replicas - 1, tile_rows * keep, tile_cols)
     output = output_pass(
         next_hidden, down_weight, mine, values, indices, spread, mats, chunk, size
     )

time: 67.9 us -> 65.4 us (0.963)
  local copies, waits for them, and re-layouts: 6.95 us -> 2.21 us
  Pallas kernels: 58.3 us -> 60.5 us
    pallas_call x1, Pallas kernels: 15.9 us -> 22.1 us  [output_pass(): pl.pallas_call(functools.partial(output_kernel, chunk, size), grid=(steps...]
    unnamed x3 -> x2, local copies, waits for them, and re-layouts: 6.94 us -> 2.21 us
    pallas_call x1, Pallas kernels: 18.6 us -> 14.6 us  [moment_pass(): pl.pallas_call(functools.partial(moment_kernel, chunk), grid=(rows // tal...]
where the time goes in v5:
time: 65.4 us; the launch traced here: 64.9 us
  Pallas kernels  60.5 us (93%)
  local copies, waits for them, and re-layouts  2.21 us (3%)
  other arithmetic  1.49 us (2%)
  between operations  0.66 us (1%)
    pallas_call x1, Pallas kernels, hidden_pass(): pl.pallas_call(functools.partial(hidden_kernel, size), out_shape=(jax.Sha...  23.8 us
    pallas_call x1, Pallas kernels, output_pass(): pl.pallas_call(functools.partial(output_kernel, chunk, size), grid=(steps...  22.1 us
    pallas_call x1, Pallas kernels, moment_pass(): pl.pallas_call(functools.partial(moment_kernel, chunk), grid=(rows // tal...  14.6 us
    unnamed x2, local copies, waits for them, and re-layouts  2.21 us
    concatenate x1, other arithmetic, on_device(): jnp.concatenate([tokens.T, jnp.concatenate([turned[:share // 2], turned[s...  1.49 us

profile of v5, /device:TPU:0, one launch (start us, length us, event | category | flops | bytes accessed | tf_op | source)
XLA Modules:
  0.0 64.9 jit_solution(5116735013314094810)
XLA Ops:
  0.6 0.9 %copy.17 = bf16[64,160]{0,1:T(8,128)(2,1)S(1)} copy(bf16[64,160]{1,0:T(8,128)(2,1)} %param.16) | data formatting | bytes 40960 | tf_op args[1]
  1.5 1.5 %maximum_maximum_fusion.feature_block = bf16[240,128]{1,0:T(8,128)(2,1)} fusion(bf16[80,64]{1,0:T(8,128)(2,1)S(1)} %get-tuple-element.15, bf16[80,64]{1,0:T(8,128)(2,1)S(1)} %get-tuple-element.14, bf16[160,128]{1,0:T(8,128)(2,1)} %bitcast.9), kind=kLoop, calls=%fused_computation | loop fusion | flops 184320 | bytes 122880 | tf_op jit(solution)/shard_map/concatenate | solution.py:456
  3.0 23.8 %hidden_pass.1 = (bf16[16,160,128]{2,1,0:T(8,128)(2,1)}, bf16[896,128]{1,0:T(8,128)(2,1)}, bf16[896,64]{1,0:T(8,128)(2,1)}) custom-call(bf16[240,128]{1,0:T(8,128)(2,1)} %maximum_maximum_fusion.feature_block, bf16[160,128]{1,0:T(8,128)(2,1)} %bitcast.10, bf16[2560,896]{1,0:T(8,128)(2,1)} %gate_weight.1, bf16[2560,896]{1,0:T(8,128)(2,1)} %up_weight.1), custom_call_target="tpu_custom_call" | custom-call | tf_op jit(solution)/shard_map/hidden_pass/pallas_call | solution.py:157
  26.8 14.6 %moment_pass.1 = (bf16[1,896,2560]{2,1,0:T(8,128)(2,1)}, bf16[896,2560]{1,0:T(8,128)(2,1)}, bf16[448,40]{1,0:T(8,128)(2,1)}) custom-call(bf16[896,128]{1,0:T(8,128)(2,1)} %get-tuple-element.9.hidden, bf16[2560,128]{1,0:T(8,128)(2,1)} %bitcast.7, bf16[1,896,2560]{2,1,0:T(8,128)(2,1)} %momentum.1, s32[2,14,32,40]{3,2,1,0:T(8,128)} %bitcast.5, ...), custom_call_target="tpu_custom_call" | custom-call | tf_op jit(solution)/shard_map/moment_pass/pallas_call | solution.py:259
  41.4 22.1 %output_pass.1 = bf16[4,2560]{1,0:T(4,128)(2,1)} custom-call(bf16[896,64]{1,0:T(8,128)(2,1)} %get-tuple-element.8.hidden, bf16[896,2560]{1,0:T(8,128)(2,1)} %down.1, bf16[896,2560]{1,0:T(8,128)(2,1)} %get-tuple-element.11.mine, bf16[448,40]{1,0:T(8,128)(2,1)} %get-tuple-element.12.values, s32[2,14,32,40]{3,2,1,0:T(8,128)} %bitcast.6, ...), custom_call_target="tpu_custom_call" | custom-call | tf_op jit(solution)/shard_map/output_pass/pallas_call | solution.py:410
  63.6 1.3 %copy.19 = bf16[4,2560]{1,0:T(4,128)(2,1)} copy(bf16[4,2560]{1,0:T(4,128)(2,1)} %output_pass.1) | data formatting | bytes 40960
  (1 shorter events, 0.0 us)
